TPU v7x, 32 devices: a whole 2x2x4 slice. The times are simulated.
32 devices in a mesh: dp: 8 (over y, x, core), tensor: 4 (over z).
Axes of the slice: x: 2, y: 2, z: 4, core: 2. Of those that a mesh axis runs over, the one named last changes fastest.
Arguments:
- inputs: bfloat16 [16384, 768], P(('dp', 'tensor')), may hold values from -6 to 6
- doc_ids: int32 [8, 2048], P('dp'), may hold values from 0 to 2, never falling along the last dimension, each value on 1 to 1024 neighbouring positions
- gain_attn: bfloat16 [768], P('dp'), may hold values from 0.099609375 to 1.8984375
- w_qkv: bfloat16 [3, 768, 768], P(None, 'dp', 'tensor'), may hold values from -0.3125 to 0.3125
- w_out: bfloat16 [768, 768], P('tensor', 'dp'), may hold values from -1.75 to 1.75
- gain_mlp: bfloat16 [768], P('dp'), may hold values from 0.099609375 to 1.8984375
- w_up: bfloat16 [768, 3072], P('dp', 'tensor'), may hold values from -0.21875 to 0.21875
- w_down: bfloat16 [3072, 768], P('tensor', 'dp'), may hold values from -0.109375 to 0.109375
- grad_out: bfloat16 [16384, 768], P(('dp', 'tensor')), may hold values from -6 to 6
Outputs:
- layer_out: bfloat16 [16384, 768], P(('dp', 'tensor'))
- grad_inputs: float32 [16384, 768], P(('dp', 'tensor'))
- grad_gain_attn: float32 [768], P('dp')
- grad_w_qkv: float32 [3, 768, 768], P(None, 'dp', 'tensor')
- grad_w_out: float32 [768, 768], P('tensor', 'dp')
- grad_gain_mlp: float32 [768], P('dp')
- grad_w_up: float32 [768, 3072], P('dp', 'tensor')
- grad_w_down: float32 [3072, 768], P('tensor', 'dp')
Inputs may be any that keep to these rules, and one draw needn't show every extreme that they name: `doc_ids`: each row holds the 3 documents of one group in order, each of one or more positions, the longest exactly 1024 positions.
All inputs are finite; a program needn't handle non-finite values.
Results may differ from a plain program's by a relative error of at most 0.015.
The roundings to bfloat16 on the way count: a program that leaves them out, or rounds other values in their place, can miss the bound.
Values may be sent and summed in bfloat16 or wider, within the bound.
No kernel may reach another device: no remote copies, remote signals or barrier semaphores. Data moves between devices by JAX's collectives and lax.ppermute only.
A program may use at most 192 MiB of HBM per device.

v0:
```python
import jax
import jax.numpy as jnp
from jax import lax
from jax.sharding import PartitionSpec as P

HEAD_DIM = 64
BLOCK = 256


eps = 1e-05


def norm_rows(row_data, gain):
    row_mean = jnp.mean(row_data, axis=-1, keepdims=True)
    centered = row_data - row_mean
    variance = jnp.mean(centered * centered, axis=-1, keepdims=True)
    return centered * lax.rsqrt(variance + eps) * gain


def gelu_tanh(values):
    return (
        0.5
        * values
        * (1.0 + jnp.tanh(0.7978845608028654 * (values + 0.044715 * values * values * values)))
    )


def cog_weights(scores, visible):
    absolute = jnp.abs(scores)
    largest = jnp.max(jnp.where(visible, absolute, 0.0), axis=-1, keepdims=True)
    summed = jnp.sum(jnp.where(visible, jnp.exp(absolute - largest), 0.0), axis=-1, keepdims=True)
    log_total = largest + jnp.log(summed)
    magnitude = jnp.where(visible, jnp.exp(absolute - log_total), 0.0)
    return (jnp.sign(scores) * magnitude, log_total)


def cog_parts(scores, visible, log_total):
    magnitude = jnp.where(visible, jnp.exp(jnp.abs(scores) - log_total), 0.0)
    return (jnp.sign(scores) * magnitude, magnitude)


def visible_mask(documents, row_start, row_count, extent):
    query_places = row_start + jnp.arange(row_count, dtype=jnp.int32)
    key_places = jnp.arange(extent, dtype=jnp.int32)
    same_doc = documents[row_start:extent][:, None] == documents[:extent][None, :]
    return same_doc & (key_places[None, :] // BLOCK <= query_places[:, None] // BLOCK)


def attention_forward(queries, key_rows, value_rows, documents):
    head_count = queries.shape[0]
    token_count = queries.shape[1]
    row_count = min(512, token_count)
    score_scale = HEAD_DIM ** (-0.5)
    head_pieces = [[] for head_index in range(head_count)]
    saved_totals = []
    for block_index in range(token_count // row_count):
        row_start = block_index * row_count
        extent = row_start + row_count
        visible = visible_mask(documents, row_start, row_count, extent)
        for head_index in range(head_count):
            scores = (
                jnp.einsum(
                    "qd,kd->qk",
                    queries[head_index, row_start:extent],
                    key_rows[head_index, :extent],
                    preferred_element_type=jnp.float32,
                )
                * score_scale
            )
            weights, log_total = cog_weights(scores, visible)
            head_pieces[head_index].append(
                jnp.dot(
                    weights.astype(jnp.bfloat16),
                    value_rows[head_index, :extent],
                    preferred_element_type=jnp.float32,
                )
            )
            saved_totals.append(log_total)
    result = jnp.concatenate([jnp.concatenate(pieces, axis=0) for pieces in head_pieces], axis=1)
    return (result, saved_totals)


def attention_backward(queries, key_rows, value_rows, documents, saved_totals, grad_heads):
    head_count = queries.shape[0]
    token_count = queries.shape[1]
    row_count = min(512, token_count)
    score_scale = HEAD_DIM ** (-0.5)
    query_pieces = [[] for head_index in range(head_count)]
    grad_keys = jnp.zeros(queries.shape, jnp.float32)
    grad_values = jnp.zeros(queries.shape, jnp.float32)
    position = 0
    for block_index in range(token_count // row_count):
        row_start = block_index * row_count
        extent = row_start + row_count
        visible = visible_mask(documents, row_start, row_count, extent)
        for head_index in range(head_count):
            query_block = queries[head_index, row_start:extent]
            grad_block = grad_heads[head_index, row_start:extent]
            scores = (
                jnp.einsum(
                    "qd,kd->qk",
                    query_block,
                    key_rows[head_index, :extent],
                    preferred_element_type=jnp.float32,
                )
                * score_scale
            )
            weights, magnitude = cog_parts(scores, visible, saved_totals[position])
            position += 1
            pushed = jnp.einsum(
                "qd,kd->qk",
                grad_block,
                value_rows[head_index, :extent],
                preferred_element_type=jnp.float32,
            )
            inner_sum = jnp.sum(pushed * weights, axis=-1, keepdims=True)
            grad_scores = (magnitude * pushed - weights * inner_sum).astype(jnp.bfloat16)
            query_pieces[head_index].append(
                jnp.dot(
                    grad_scores, key_rows[head_index, :extent], preferred_element_type=jnp.float32
                )
                * score_scale
            )
            grad_keys = grad_keys.at[head_index, :extent].add(
                jnp.einsum(
                    "qk,qd->kd", grad_scores, query_block, preferred_element_type=jnp.float32
                )
                * score_scale
            )
            grad_values = grad_values.at[head_index, :extent].add(
                jnp.einsum(
                    "qk,qd->kd",
                    weights.astype(jnp.bfloat16),
                    grad_block,
                    preferred_element_type=jnp.float32,
                )
            )
    grad_queries = jnp.stack([jnp.concatenate(pieces, axis=0) for pieces in query_pieces])
    return (grad_queries, grad_keys, grad_values)


def shards(inputs, doc_ids, gain_attn, w_qkv, w_out, gain_mlp, w_up, w_down, grad_out):
    documents = doc_ids[0]
    gathered = (
        lax.all_gather(gain_attn, "dp", axis=0, tiled=True),
        lax.all_gather(w_qkv, "dp", axis=1, tiled=True),
        lax.all_gather(w_out, "dp", axis=1, tiled=True),
        lax.all_gather(gain_mlp, "dp", axis=0, tiled=True),
        lax.all_gather(w_up, "dp", axis=0, tiled=True),
        lax.all_gather(w_down, "dp", axis=1, tiled=True),
    )
    gain_one = gathered[0].astype(jnp.float32)
    full_qkv = gathered[1]
    full_out = gathered[2]
    gain_two = gathered[3].astype(jnp.float32)
    full_up = gathered[4]
    full_down = gathered[5]
    head_count = full_qkv.shape[2] // HEAD_DIM
    input_rows = inputs.astype(jnp.float32)
    normed_rows = norm_rows(input_rows, gain_one).astype(jnp.bfloat16)
    normed_all = lax.all_gather(normed_rows, "tensor", axis=0, tiled=True)
    token_count = normed_all.shape[0]
    projected = jnp.einsum(
        "td,cde->cte", normed_all, full_qkv, preferred_element_type=jnp.float32
    ).astype(jnp.bfloat16)
    by_head = projected.reshape(3, token_count, head_count, HEAD_DIM).transpose(0, 2, 1, 3)
    attended_f, saved_totals = attention_forward(by_head[0], by_head[1], by_head[2], documents)
    attended = attended_f.astype(jnp.bfloat16)
    attn_rows = lax.psum_scatter(
        jnp.dot(attended, full_out, preferred_element_type=jnp.float32),
        "tensor",
        scatter_dimension=0,
        tiled=True,
    )
    mixed_rows = input_rows + attn_rows
    mlp_rows = norm_rows(mixed_rows, gain_two).astype(jnp.bfloat16)
    mlp_all = lax.all_gather(mlp_rows, "tensor", axis=0, tiled=True)
    hidden = jnp.dot(mlp_all, full_up, preferred_element_type=jnp.float32)
    active = gelu_tanh(hidden).astype(jnp.bfloat16)
    layer_out = (
        mixed_rows
        + lax.psum_scatter(
            jnp.dot(active, full_down, preferred_element_type=jnp.float32).astype(jnp.bfloat16),
            "tensor",
            scatter_dimension=0,
            tiled=True,
        ).astype(jnp.float32)
    ).astype(jnp.bfloat16)
    regathered = (
        lax.all_gather(w_qkv, "dp", axis=1, tiled=True),
        lax.all_gather(w_out, "dp", axis=1, tiled=True),
        lax.all_gather(w_up, "dp", axis=0, tiled=True),
        lax.all_gather(w_down, "dp", axis=1, tiled=True),
    )
    full_qkv = regathered[0]
    full_out = regathered[1]
    full_up = regathered[2]
    full_down = regathered[3]
    cotangent = lax.all_gather(grad_out, "tensor", axis=0, tiled=True)
    grad_down = jnp.einsum("tf,td->fd", active, cotangent, preferred_element_type=jnp.float32)
    grad_active = jnp.einsum("td,fd->tf", cotangent, full_down, preferred_element_type=jnp.float32)
    gelu_value, gelu_pull = jax.vjp(gelu_tanh, hidden)
    grad_hidden = gelu_pull(grad_active)[0].astype(jnp.bfloat16)
    mlp_all = lax.all_gather(mlp_rows, "tensor", axis=0, tiled=True)
    grad_up = jnp.einsum("td,tf->df", mlp_all, grad_hidden, preferred_element_type=jnp.float32)
    grad_mlp_rows = lax.psum_scatter(
        jnp.einsum("tf,df->td", grad_hidden, full_up, preferred_element_type=jnp.float32),
        "tensor",
        scatter_dimension=0,
        tiled=True,
    )
    norm_value, second_pull = jax.vjp(norm_rows, mixed_rows, gain_two)
    grad_mixed_ln, grad_gain_two = second_pull(grad_mlp_rows)
    grad_mixed = grad_out.astype(jnp.float32) + grad_mixed_ln
    grad_branch = lax.all_gather(grad_mixed.astype(jnp.bfloat16), "tensor", axis=0, tiled=True)
    grad_outproj = jnp.einsum(
        "te,td->ed", attended, grad_branch, preferred_element_type=jnp.float32
    )
    grad_attended = jnp.einsum(
        "td,ed->te", grad_branch, full_out, preferred_element_type=jnp.float32
    ).astype(jnp.bfloat16)
    grad_heads = grad_attended.reshape(token_count, head_count, HEAD_DIM).transpose(1, 0, 2)
    grad_queries, grad_keys, grad_values = attention_backward(
        by_head[0], by_head[1], by_head[2], documents, saved_totals, grad_heads
    )
    grad_projected = (
        jnp.stack([grad_queries, grad_keys, grad_values])
        .transpose(0, 2, 1, 3)
        .reshape(3, token_count, head_count * HEAD_DIM)
        .astype(jnp.bfloat16)
    )
    normed_all = lax.all_gather(normed_rows, "tensor", axis=0, tiled=True)
    grad_proj = jnp.einsum(
        "td,cte->cde", normed_all, grad_projected, preferred_element_type=jnp.float32
    )
    grad_normed = lax.psum_scatter(
        jnp.einsum(
            "cte,cde->td", grad_projected, full_qkv, preferred_element_type=jnp.float32
        ).astype(jnp.bfloat16),
        "tensor",
        scatter_dimension=0,
        tiled=True,
    ).astype(jnp.float32)
    first_value, first_pull = jax.vjp(norm_rows, input_rows, gain_one)
    grad_input_ln, grad_gain_one = first_pull(grad_normed)
    grad_inputs = grad_mixed + grad_input_ln
    owned = (
        lax.psum_scatter(grad_proj, "dp", scatter_dimension=1, tiled=True),
        lax.psum_scatter(grad_outproj, "dp", scatter_dimension=1, tiled=True),
        lax.psum_scatter(grad_up, "dp", scatter_dimension=0, tiled=True),
        lax.psum_scatter(grad_down, "dp", scatter_dimension=1, tiled=True),
        lax.psum_scatter(grad_gain_one, "dp", scatter_dimension=0, tiled=True),
        lax.psum_scatter(grad_gain_two, "dp", scatter_dimension=0, tiled=True),
    )
    gain_totals = lax.psum((owned[4], owned[5]), "tensor")
    return (
        layer_out,
        grad_inputs,
        gain_totals[0],
        owned[0],
        owned[1],
        gain_totals[1],
        owned[2],
        owned[3],
    )


def solution(mesh):
    return jax.shard_map(
        shards,
        mesh=mesh,
        in_specs=(
            P(("dp", "tensor"), None),
            P("dp", None),
            P("dp"),
            P(None, "dp", "tensor"),
            P("tensor", "dp"),
            P("dp"),
            P("dp", "tensor"),
            P("tensor", "dp"),
            P(("dp", "tensor"), None),
        ),
        out_specs=(
            P(("dp", "tensor"), None),
            P(("dp", "tensor"), None),
            P("dp"),
            P(None, "dp", "tensor"),
            P("tensor", "dp"),
            P("dp"),
            P("dp", "tensor"),
            P("tensor", "dp"),
        ),
        check_vma=False,
    )
```

profile of v0, /device:TPU:0, one launch (start us, length us, event | category | flops | bytes accessed | tf_op | source)
XLA Modules:
  0.0 1009.0 jit_solution(13346430030188837939)
XLA Ops:
  14.7 15.7 %all-reduce.8 = (bf16[768]{0:T(1024)(128)(2,1)S(1)}, bf16[768]{0:T(1024)(128)(2,1)}) all-reduce(bf16[768]{0:T(1024)(128)(2,1)S(1)} %dynamic-update-slice.74, bf16[768]{0:T(1024)(128)(2,1)S(1)} %dynamic-update-slice.75), channel_id=1, replica_groups=mesh['dp'=8,'tensor'=4] {'dp'}, use_global_device_ids=true, to_apply=%add.2 | all-reduce | flops 1536 | bytes 6144
  33.6 12.2 %all_gather.38 = bf16[3,768,192]{2,0,1:T(4,128)(2,1)S(1)} all-gather(bf16[3,96,192]{2,0,1:T(4,128)(2,1)S(1)} %copy.20), channel_id=1, replica_groups=mesh['dp'=8,'tensor'=4] {'dp'}, dimensions={1}, use_global_device_ids=true | all-gather | bytes 995328 | tf_op jit(solution)/shard_map/all_gather | solution.py:146
  46.7 8.7 all_gather.39
  59.1 36.6 %all-gather.7.cloned.1.call-done = bf16[2048,768]{1,0:T(8,128)(2,1)} async-done(((bf16[512,768]{1,0:T(8,128)(2,1)}), bf16[2048,768]{1,0:T(8,128)(2,1)}) %all-gather.7.cloned.1.call-update) | async-done | bytes 3145744 | tf_op jit(solution)/shard_map/all_gather | solution.py:161
  95.7 3.9 fusion.162
  153.1 140.5 %reduce-scatter.13.cloned.1.call-done = f32[512,768]{1,0:T(8,128)} async-done(((f32[2048,768]{1,0:T(8,128)}), f32[512,768]{1,0:T(8,128)}) %reduce-scatter.13.cloned.1.call-update) | async-done | bytes 1572880 | tf_op jit(solution)/shard_map/reduce_scatter | solution.py:169
  298.9 11.2 %all-gather.15.cloned.1.call-done = bf16[2048,768]{1,0:T(8,128)(2,1)} async-done(((bf16[512,768]{1,0:T(8,128)(2,1)}), bf16[2048,768]{1,0:T(8,128)(2,1)}) %all-gather.15.cloned.1.call-update) | async-done | bytes 3145744 | tf_op jit(solution)/shard_map/all_gather | solution.py:199
  310.1 7.5 fusion.163
  317.6 17.8 %all-gather.11.cloned.1.call-done = bf16[768,768]{1,0:T(8,128)(2,1)} async-done(((bf16[96,768]{1,0:T(8,128)(2,1)}), bf16[768,768]{1,0:T(8,128)(2,1)}) %all-gather.11.cloned.1.call-update) | async-done | bytes 1179664 | tf_op jit(solution)/shard_map/all_gather | solution.py:149
  335.4 65.5 %all-gather.9.cloned.1.call-done = bf16[2048,768]{1,0:T(8,128)(2,1)} async-done(((bf16[512,768]{1,0:T(8,128)(2,1)}), bf16[2048,768]{1,0:T(8,128)(2,1)}) %all-gather.9.cloned.1.call-update) | async-done | bytes 3145744 | tf_op jit(solution)/shard_map/all_gather | solution.py:177
  400.9 12.3 %fusion.3 = (bf16[2048,768]{1,0:T(8,128)(2,1)S(1)}, f32[2048,768]{1,0:T(8,128)}) fusion(f32[2048,768]{1,0:T(8,128)} %fusion.163, bf16[2048,768]{1,0:T(8,128)(2,1)} %all-gather.9.cloned.1.call-done, bf16[768,768]{1,0:T(8,128)(2,1)} %all-gather.11.cloned.1.call-done), kind=kOutput, calls=%fused_computation.7 | convolution fusion | flops 2453667840 | bytes 20054016 | tf_op jit(solution)/shard_map/dot_general | solution.py:178
  414.8 4.5 fusion.164
  419.4 8.6 convolution_convert_fusion
  428.3 100.6 %reduce-scatter.17.cloned.1.call-done = f32[512,768]{1,0:T(8,128)} async-done(((f32[2048,768]{1,0:T(8,128)}), f32[512,768]{1,0:T(8,128)}) %reduce-scatter.17.cloned.1.call-update) | async-done | bytes 1572880 | tf_op jit(solution)/shard_map/reduce_scatter | solution.py:206
  532.5 59.7 %reduce-scatter.15.cloned.1.call-done = bf16[512,768]{1,0:T(8,128)(2,1)} async-done(((bf16[2048,768]{1,0:T(8,128)(2,1)}), bf16[512,768]{1,0:T(8,128)(2,1)}) %reduce-scatter.15.cloned.1.call-update) | async-done | bytes 786448 | tf_op jit(solution)/shard_map/reduce_scatter | solution.py:182
  598.2 63.4 %all-gather.17.cloned.1.call-done = bf16[2048,768]{1,0:T(8,128)(2,1)} async-done(((bf16[512,768]{1,0:T(8,128)(2,1)}), bf16[2048,768]{1,0:T(8,128)(2,1)}) %all-gather.17.cloned.1.call-update) | async-done | bytes 3145744 | tf_op jit(solution)/shard_map/all_gather | solution.py:215
  686.5 3.8 fusion.110
  718.9 6.5 multiply_reduce_fusion.6
  725.4 6.1 subtract_convert_fusion.6
  738.7 7.5 multiply_reduce_fusion.3
  746.1 7.4 subtract_convert_fusion.3
  760.8 11.4 %multiply_reduce_fusion = (f32[512]{0:T(512)S(1)}, f32[512]{0:T(512)S(1)}, f32[512]{0:T(512)S(1)}, f32[512,2048]{1,0:T(8,128)}) fusion(f32[512]{0:T(512)S(1)} %copy-done.128, f32[512,2048]{1,0:T(8,128)S(1)} %copy-done.3, s32[512]{0:T(512)S(1)} %copy-done.107, s32[2048]{0:T(1024)S(1)} %copy-done.73, s32[2048]{0:T(1024)S(1)} %bitcast.541, ...), kind=kOutput, calls=%fused_computation.13 | convolution fusion | flops 162527744 | bytes 25526272 | tf_op jit(solution)/shard_map/qd,kd->qk/dot_general | solution.py:110
  772.2 12.7 %subtract_convert_fusion = (bf16[512,2048]{1,0:T(8,128)(2,1)S(1)}, bf16[512,2048]{1,0:T(8,128)(2,1)S(1)}, bf16[512,2048]{1,0:T(8,128)(2,1)S(1)}) fusion(f32[512,2048]{1,0:T(8,128)} %get-tuple-element.400, f32[512,2048]{1,0:T(8,128)S(1)} %copy-done.3, f32[512]{0:T(512)S(1)} %get-tuple-element.316, f32[512]{0:T(512)S(1)} %copy-done.129, ...), kind=kLoop, calls=%fused_computation.12 | loop fusion | flops 34603008 | bytes 31490048 | tf_op jit(solution)/shard_map/convert_element_type | solution.py:117
  808.0 6.2 bitcast_convert_fusion
  814.3 7.4 fusion.165
  821.9 7.3 fusion.157
  831.8 15.0 %reduce-scatter.25.cloned.1.call-done = f32[96,576]{1,0:T(8,128)} async-done(((f32[768,576]{1,0:T(8,128)}), f32[96,576]{1,0:T(8,128)}) %reduce-scatter.25.cloned.1.call-update) | async-done | bytes 221200
  848.7 60.7 %reduce-scatter.19.cloned.1.call-done = bf16[512,768]{1,0:T(8,128)(2,1)} async-done(((bf16[2048,768]{1,0:T(8,128)(2,1)}), bf16[512,768]{1,0:T(8,128)(2,1)}) %reduce-scatter.19.cloned.1.call-update) | async-done | bytes 786448 | tf_op jit(solution)/shard_map/reduce_scatter | solution.py:236
  913.2 13.4 %all-reduce.6 = (f32[768]{0:T(1024)S(1)}, f32[768]{0:T(1024)S(1)}) all-reduce(f32[768]{0:T(1024)S(1)} %get-tuple-element.314, f32[768]{0:T(1024)S(1)} %copy-done.120), channel_id=6, replica_groups=mesh['dp'=8,'tensor'=4] {'dp'}, use_global_device_ids=true, to_apply=%region_49.50.clone | all-reduce | flops 1536 | bytes 12288
  926.7 11.4 %all-reduce.7 = (f32[96]{0:T(128)}, f32[96]{0:T(128)}) all-reduce(f32[96]{0:T(128)S(1)} %dynamic-slice.195, f32[96]{0:T(128)S(1)} %dynamic-slice.197), channel_id=1, replica_groups=mesh['dp'=8,'tensor'=4] {'tensor'}, use_global_device_ids=true, to_apply=%region_50.51 | all-reduce | flops 192 | bytes 1536 | tf_op jit(solution)/shard_map/psum | solution.py:255
  941.1 14.3 %reduce-scatter.21.cloned.1.call-done = f32[96,768]{1,0:T(8,128)} async-done(((f32[768,768]{1,0:T(8,128)}), f32[96,768]{1,0:T(8,128)}) %reduce-scatter.21.cloned.1.call-update) | async-done | bytes 294928 | tf_op jit(solution)/shard_map/reduce_scatter | solution.py:250
  955.4 46.0 %reduce-scatter.23.cloned.1.call-done = f32[768,96]{0,1:T(8,128)} async-done(((f32[768,768]{0,1:T(8,128)}), f32[768,96]{0,1:T(8,128)}) %reduce-scatter.23.cloned.1.call-update) | async-done | bytes 294928 | tf_op jit(solution)/shard_map/reduce_scatter | solution.py:251
  (510 shorter events, 183.5 us)
Async XLA Ops:
  8.0 87.7 %all-gather.7.cloned.1.call-start = ((), (), s32[]{:S(2)}) async-start(), calls=%async_computation.8 | async-start | bytes 3932160 | tf_op jit(solution)/shard_map/all_gather | solution.py:161
  9.4 36.4 %copy-start.70 = (f32[512]{0:T(512)}, f32[512]{0:T(512)S(1)}, u32[]{:S(2)}) copy-start(f32[512]{0:T(512)S(1)} %broadcast_multiply_fusion.1) | copy-start | bytes 6148
  11.0 34.9 %copy-start.93 = (f32[512]{0:T(512)}, f32[512]{0:T(512)S(1)}, u32[]{:S(2)}) copy-start(f32[512]{0:T(512)S(1)} %fusion.148) | copy-start | bytes 6148
  32.7 260.9 %reduce-scatter.13.cloned.1.call-start = ((), (), s32[]{:S(2)}) async-start(), calls=%async_computation.9 | async-start | bytes 7864320 | tf_op jit(solution)/shard_map/reduce_scatter | solution.py:169
  46.7 52.9 %copy-start.57 = (bf16[3,768,192]{1,2,0:T(8,128)(2,1)}, bf16[3,768,192]{1,2,0:T(8,128)(2,1)S(1)}, u32[]{:S(2)}) copy-start(bf16[3,768,192]{1,2,0:T(8,128)(2,1)S(1)} %copy.21) | copy-start | bytes 2654212
  100.0 42.7 %copy-start.8 = (bf16[2048,3,192]{0,2,1:T(8,128)(2,1)}, bf16[2048,3,192]{0,2,1:T(8,128)(2,1)S(1)}, u32[]{:S(2)}) copy-start(bf16[2048,3,192]{0,2,1:T(8,128)(2,1)S(1)} %convert_element_type.146) | copy-start | bytes 7077892
  102.4 34.4 %copy-start.2 = (f32[512,2048]{1,0:T(8,128)}, f32[512,2048]{1,0:T(8,128)S(1)}, u32[]{:S(2)}) copy-start(f32[512,2048]{1,0:T(8,128)S(1)} %fusion.113) | copy-start | bytes 12582916
  105.1 40.5 %copy-start.148 = (bf16[512,64]{0,1:T(8,128)(2,1)}, bf16[512,64]{0,1:T(8,128)(2,1)S(1)}, u32[]{:S(2)}) copy-start(bf16[512,64]{0,1:T(8,128)(2,1)S(1)} %convolution_convert_fusion.5) | copy-start | bytes 196612
  105.8 39.8 %copy-start.150 = (bf16[512,64]{0,1:T(8,128)(2,1)}, bf16[512,64]{0,1:T(8,128)(2,1)S(1)}, u32[]{:S(2)}) copy-start(bf16[512,64]{0,1:T(8,128)(2,1)S(1)} %convolution_convert_fusion.6) | copy-start | bytes 196612
  106.5 39.1 %copy-start.152 = (bf16[512,64]{0,1:T(8,128)(2,1)}, bf16[512,64]{0,1:T(8,128)(2,1)S(1)}, u32[]{:S(2)}) copy-start(bf16[512,64]{0,1:T(8,128)(2,1)S(1)} %convolution_convert_fusion.7) | copy-start | bytes 196612
  112.9 32.7 %copy-start.154 = (bf16[512,64]{0,1:T(8,128)(2,1)}, bf16[512,64]{0,1:T(8,128)(2,1)S(1)}, u32[]{:S(2)}) copy-start(bf16[512,64]{0,1:T(8,128)(2,1)S(1)} %convolution_convert_fusion.2) | copy-start | bytes 196612
  114.5 31.1 %copy-start.156 = (bf16[512,64]{0,1:T(8,128)(2,1)}, bf16[512,64]{0,1:T(8,128)(2,1)S(1)}, u32[]{:S(2)}) copy-start(bf16[512,64]{0,1:T(8,128)(2,1)S(1)} %convolution_convert_fusion.3) | copy-start | bytes 196612
  150.0 148.8 %all-gather.13.cloned.1.call-start = ((), (), s32[]{:S(2)}) async-start(), calls=%async_computation.12 | async-start | bytes 1327104 | tf_op jit(solution)/shard_map/all_gather | solution.py:150
  150.6 159.5 %all-gather.15.cloned.1.call-start = ((), (), s32[]{:S(2)}) async-start(), calls=%async_computation.14 | async-start | bytes 3932160 | tf_op jit(solution)/shard_map/all_gather | solution.py:199
  151.2 184.2 %all-gather.11.cloned.1.call-start = ((), (), s32[]{:S(2)}) async-start(), calls=%async_computation.11 | async-start | bytes 1327104 | tf_op jit(solution)/shard_map/all_gather | solution.py:149
  151.8 249.1 %all-gather.9.cloned.1.call-start = ((), (), s32[]{:S(2)}) async-start(), calls=%async_computation.10 | async-start | bytes 3932160 | tf_op jit(solution)/shard_map/all_gather | solution.py:177
  298.4 230.5 %reduce-scatter.17.cloned.1.call-start = ((), (), s32[]{:S(2)}) async-start(), calls=%async_computation.15 | async-start | bytes 7864320 | tf_op jit(solution)/shard_map/reduce_scatter | solution.py:206
  419.4 172.7 %reduce-scatter.15.cloned.1.call-start = ((), (), s32[]{:S(2)}) async-start(), calls=%async_computation.13 | async-start | bytes 3932160 | tf_op jit(solution)/shard_map/reduce_scatter | solution.py:182
  428.0 233.5 %all-gather.17.cloned.1.call-start = ((), (), s32[]{:S(2)}) async-start(), calls=%async_computation.16 | async-start | bytes 3932160 | tf_op jit(solution)/shard_map/all_gather | solution.py:215
  598.1 231.9 %reduce-scatter.27.cloned.1.call-start = ((), (), s32[]{:S(2)}) async-start(), calls=%async_computation.21 | async-start | bytes 884736
  692.8 154.1 %reduce-scatter.25.cloned.1.call-start = ((), (), s32[]{:S(2)}) async-start(), calls=%async_computation.20 | async-start | bytes 2211840
  807.9 101.4 %reduce-scatter.19.cloned.1.call-start = ((), (), s32[]{:S(2)}) async-start(), calls=%async_computation.17 | async-start | bytes 3932160 | tf_op jit(solution)/shard_map/reduce_scatter | solution.py:236
  814.2 141.2 %reduce-scatter.21.cloned.1.call-start = ((), (), s32[]{:S(2)}) async-start(), calls=%async_computation.18 | async-start | bytes 2654208 | tf_op jit(solution)/shard_map/reduce_scatter | solution.py:250
  821.7 179.8 %reduce-scatter.23.cloned.1.call-start = ((), (), s32[]{:S(2)}) async-start(), calls=%async_computation.19 | async-start | bytes 2654208 | tf_op jit(solution)/shard_map/reduce_scatter | solution.py:251
  829.3 80.1 %copy-start.1 = (bf16[512,768]{1,0:T(8,128)(2,1)S(1)}, bf16[512,768]{1,0:T(8,128)(2,1)}, u32[]{:S(2)}) copy-start(bf16[512,768]{1,0:T(8,128)(2,1)} %param.57) | copy-start | bytes 2359300
  829.3 80.1 %copy-start.69 = (f32[768]{0:T(1024)S(1)}, f32[768]{0:T(1024)}, u32[]{:S(2)}) copy-start(f32[768]{0:T(1024)} %copy-done.68) | copy-start | bytes 9220
  829.3 80.1 %copy-start.71 = (f32[512]{0:T(512)S(1)}, f32[512]{0:T(512)}, u32[]{:S(2)}) copy-start(f32[512]{0:T(512)} %copy-done.70) | copy-start | bytes 6148
  829.3 81.8 %copy-start.111 = (f32[512]{0:T(512)S(1)}, f32[512]{0:T(512)}, u32[]{:S(2)}) copy-start(f32[512]{0:T(512)} %copy-done.110) | copy-start | bytes 6148
  829.3 81.8 %copy-start.94 = (f32[512]{0:T(512)S(1)}, f32[512]{0:T(512)}, u32[]{:S(2)}) copy-start(f32[512]{0:T(512)} %copy-done.93) | copy-start | bytes 6148
  829.3 83.9 %copy-start.120 = (f32[768]{0:T(1024)S(1)}, f32[768]{0:T(1024)}, u32[]{:S(2)}) copy-start(f32[768]{0:T(1024)} %get-tuple-element.312) | copy-start | bytes 9220
  830.1 108.1 %copy-start.16 = (f32[512,768]{1,0:T(8,128)S(1)}, f32[512,768]{1,0:T(8,128)}, u32[]{:S(2)}) copy-start(f32[512,768]{1,0:T(8,128)} %copy-done.15) | copy-start | bytes 4718596
  830.1 108.1 %copy-start.115 = (f32[512]{0:T(512)S(1)}, f32[512]{0:T(512)}, u32[]{:S(2)}) copy-start(f32[512]{0:T(512)} %copy-done.114) | copy-start | bytes 6148
  (148 other events, 763.8 us)
Sparse Core Ops, SparseCore 0:
  32.9 62.7 all-gather.6
  150.2 143.4 reduce-scatter.12
  598.3 63.2 all-gather.16
Sparse Core Ops, SparseCore 1:
  152.4 22.4 all-gather.12
  176.3 133.7 all-gather.14
  311.8 23.5 all-gather.10
  337.6 63.3 all-gather.8
  419.5 109.3 reduce-scatter.16
  531.2 60.9 reduce-scatter.14
  692.8 33.5 reduce-scatter.26
  808.0 38.7 reduce-scatter.24
  849.0 60.3 reduce-scatter.18
  913.3 42.0 reduce-scatter.20
  959.2 42.2 reduce-scatter.22
where the time goes:
time: 1010 us
  waiting for transfers between devices  633 us (63%)
  matrix products  193 us (19%)
  other arithmetic  71.2 us (7%)
  blocking collectives  61.4 us (6%)
  local copies, waits for them, and re-layouts  28.4 us (3%)
  between operations  19.7 us (2%)
    reduce_scatter x1, waiting for transfers between devices, shards(): lax.psum_scatter(jnp.dot(attended, full_out, preferred_element_type=jnp.f...  141 us
    reduce_scatter x1, waiting for transfers between devices, shards(): lax.psum_scatter(jnp.einsum('tf,df->td', grad_hidden, full_up, preferred_...  101 us
    all_gather x1, waiting for transfers between devices, shards(): mlp_all = lax.all_gather(mlp_rows, 'tensor', axis=0, tiled=True)  65.5 us
    all_gather x1, waiting for transfers between devices, shards(): lax.all_gather(grad_mixed.astype(jnp.bfloat16), 'tensor', axis=0, tiled=T...  63.4 us
    reduce_scatter x1, waiting for transfers between devices, shards(): lax.psum_scatter(jnp.einsum('cte,cde->td', grad_projected, full_qkv, pref...  60.7 us
    reduce_scatter x1, waiting for transfers between devices, shards(): lax.psum_scatter(jnp.dot(active, full_down, preferred_element_type=jnp.fl...  59.7 us
    reduce_scatter x1, waiting for transfers between devices, shards(): lax.psum_scatter(grad_down, 'dp', scatter_dimension=1, tiled=True)  46 us
    dot_general x12, matrix products, attention_backward(): jnp.einsum('qd,kd->qk', grad_block, value_rows[head_index, :extent], pref...  43.7 us
  transfers between devices with their start and end apart: 14, of which 12 were waited for; matrix products, arithmetic and copies ran while one was open for 17% of the time, Pallas kernels for 0%

commit v1 on v0

v1 whole, which is shorter than its diff:
```python
import functools

import jax
import jax.numpy as jnp
from jax import lax
from jax.experimental import pallas as pl
from jax.experimental.pallas import tpu as pltpu
from jax.sharding import PartitionSpec as P

HEAD_DIM = 64
BLOCK = 256
f32 = jnp.float32
bf16 = jnp.bfloat16
HIDE = -1e30


def nn(a, b):
    return lax.dot_general(a, b, (((1,), (0,)), ((), ())), preferred_element_type=f32)


def nt(a, b):
    return lax.dot_general(a, b, (((1,), (1,)), ((), ())), preferred_element_type=f32)


def doc_of(place, ends):
    return jnp.where(place >= ends[1], 2, jnp.where(place >= ends[0], 1, 0))


def first_block(row, ends):
    start = jnp.where(row >= ends[1], ends[1], jnp.where(row >= ends[0], ends[0], 0))
    return lax.div(start, BLOCK)


def hidden_bias(i, j, ends):
    keys = j * BLOCK + lax.broadcasted_iota(jnp.int32, (BLOCK, BLOCK), 0)
    rows = i * BLOCK + lax.broadcasted_iota(jnp.int32, (BLOCK, BLOCK), 1)
    return jnp.where(doc_of(keys, ends) == doc_of(rows, ends), 0.0, HIDE)


def sign_of(s):
    return jnp.clip(s * 3e38, -1.0, 1.0)


def ring_blocks(z, count):
    for n in range(count):
        yield n, lax.rem(z - n // 2 + 4, 4) * 2 + n % 2


def attn_fwd_body(scal, *refs):
    parts, (out, lse, qs, vs, ks, acc) = refs[:-6], refs[-6:]
    i = pl.program_id(0)
    width = qs.shape[1]
    heads = width // HEAD_DIM
    z = scal[0]
    ends = (scal[1], scal[2])

    @pl.when(i == 0)
    def _():
        for n, b in ring_blocks(z, len(parts)):
            ref = parts[n]
            qs[b] = ref[0:width] * bf16(0.125)
            vs[b] = ref[2 * width : 3 * width]
            for h in range(heads):
                ks[h, b] = ref[width + h * HEAD_DIM : width + (h + 1) * HEAD_DIM].T

    acc[...] = jnp.zeros_like(acc)

    def step(j, carry):
        bias = hidden_bias(i, j, ends)
        new = []
        for h in range(heads):
            rows = slice(h * HEAD_DIM, (h + 1) * HEAD_DIM)
            m, l = carry[h]
            s = nn(ks[h, j], qs[i, rows])
            a = jnp.abs(s) + bias
            m_new = jnp.maximum(m, jnp.max(a, axis=0, keepdims=True))
            p = jnp.exp(a - m_new)
            alpha = jnp.exp(m - m_new)
            w = (sign_of(s) * p).astype(bf16)
            acc[rows] = acc[rows] * alpha + nn(vs[j, rows], w)
            new.append((m_new, l * alpha + jnp.sum(p, axis=0, keepdims=True)))
        return tuple(new)

    zero = jnp.zeros((1, BLOCK), f32)
    stats = lax.fori_loop(first_block(i * BLOCK, ends), i + 1, step, ((zero, zero),) * heads)
    t = lax.div(i, 2)
    cols = pl.ds(pl.multiple_of(lax.rem(i, 2) * BLOCK, BLOCK), BLOCK)
    dest = lax.rem(t - z + 4, 4)
    for h in range(heads):
        rows = slice(h * HEAD_DIM, (h + 1) * HEAD_DIM)
        m, l = stats[h]
        out[dest, rows, cols] = (acc[rows] / l).astype(bf16)
        lse[i, h : h + 1, :] = m + jnp.log(l)


def whole(shape):
    return pl.BlockSpec(shape, lambda *_: (0,) * len(shape))


def attn_fwd(scal, parts):
    width, nb = parts[0].shape[0] // 3, len(parts)
    heads = width // HEAD_DIM
    cols = nb // 4 * BLOCK
    return pl.pallas_call(
        attn_fwd_body,
        out_shape=(
            jax.ShapeDtypeStruct((4, width, cols), bf16),
            jax.ShapeDtypeStruct((nb, 8, BLOCK), f32),
        ),
        grid_spec=pltpu.PrefetchScalarGridSpec(
            num_scalar_prefetch=1,
            grid=(nb,),
            in_specs=[whole(p.shape) for p in parts],
            out_specs=(whole((4, width, cols)), whole((nb, 8, BLOCK))),
            scratch_shapes=[
                pltpu.VMEM((nb, width, BLOCK), bf16),
                pltpu.VMEM((nb, width, BLOCK), bf16),
                pltpu.VMEM((heads, nb, BLOCK, HEAD_DIM), bf16),
                pltpu.VMEM((width, BLOCK), f32),
            ],
        ),
        compiler_params=pltpu.CompilerParams(dimension_semantics=("arbitrary",)),
        cost_estimate=pl.CostEstimate(
            flops=4 * heads * 20 * BLOCK * BLOCK * 256, bytes_accessed=4_000_000, transcendentals=heads * 20 * BLOCK * BLOCK
        ),
        name="attn_fwd",
    )(scal, *parts)


def attn_bwd_body(scal, *refs):
    parts, refs = refs[:-16], refs[-16:]
    o, g0, g1, g2, g3, lse, grad, qs, kts, gs, ks, vns, inner, dq, dk, dv = refs
    i = pl.program_id(0)
    nb = pl.num_programs(0)
    width = qs.shape[1]
    heads = width // HEAD_DIM
    z = scal[0]
    ends = (scal[1], scal[2])

    @pl.when(i == 0)
    def _():
        for n, b in ring_blocks(z, len(parts)):
            ref = parts[n]
            qs[b] = ref[0:width] * bf16(0.125)
            kts[b] = ref[width : 2 * width]
            for h in range(heads):
                ks[h, b] = ref[width + h * HEAD_DIM : width + (h + 1) * HEAD_DIM].T
                vns[h, b] = ref[2 * width + h * HEAD_DIM : 2 * width + (h + 1) * HEAD_DIM].T
        for s, ref in enumerate((g0, g1, g2, g3)):
            t = lax.rem(z + s, 4)
            for half in range(2):
                cols = slice(half * BLOCK, (half + 1) * BLOCK)
                gs[t * 2 + half] = ref[:, cols]
                both = ref[:, cols].astype(f32) * o[s, :, cols].astype(f32)
                for h in range(heads):
                    inner[t * 2 + half, h : h + 1, :] = jnp.sum(
                        both[h * HEAD_DIM : (h + 1) * HEAD_DIM], axis=0, keepdims=True
                    )
        dk[...] = jnp.zeros_like(dk)
        dv[...] = jnp.zeros_like(dv)

    dq[i] = jnp.zeros(dq.shape[1:], f32)

    def step(j, carry):
        bias = hidden_bias(i, j, ends)
        for h in range(heads):
            rows = slice(h * HEAD_DIM, (h + 1) * HEAD_DIM)
            q = qs[i, rows]
            g = gs[i, rows]
            s = nn(ks[h, j], q)
            pushed = nn(vns[h, j], g)
            mag = jnp.exp(jnp.abs(s) + bias - lse[i, h : h + 1, :])
            w = sign_of(s) * mag
            ds = (mag * pushed - w * inner[i, h : h + 1, :]).astype(bf16)
            dv[j, rows] += nt(g, w.astype(bf16))
            dk[j, rows] += nt(q, ds)
            dq[i, rows] += nn(kts[j, rows], ds)
        return carry

    lax.fori_loop(first_block(i * BLOCK, ends), i + 1, step, 0)

    @pl.when(i == nb - 1)
    def _():
        for n, b in ring_blocks(z, len(parts)):
            cols = slice(n * BLOCK, (n + 1) * BLOCK)
            grad[0:width, cols] = (dq[b] * 0.125).astype(bf16)
            grad[width : 2 * width, cols] = dk[b].astype(bf16)
            grad[2 * width : 3 * width, cols] = dv[b].astype(bf16)


def attn_bwd(scal, parts, attended, grads, lse):
    width, nb = parts[0].shape[0] // 3, len(parts)
    heads = width // HEAD_DIM
    cols = nb // 4 * BLOCK
    block16 = pltpu.VMEM((nb, width, BLOCK), bf16)
    natural = pltpu.VMEM((heads, nb, BLOCK, HEAD_DIM), bf16)
    block32 = pltpu.VMEM((nb, width, BLOCK), f32)
    ops = (*parts, attended, *grads, lse)
    return pl.pallas_call(
        attn_bwd_body,
        out_shape=jax.ShapeDtypeStruct((3 * width, nb * BLOCK), bf16),
        grid_spec=pltpu.PrefetchScalarGridSpec(
            num_scalar_prefetch=1,
            grid=(nb,),
            in_specs=[whole(p.shape) for p in ops],
            out_specs=whole((3 * width, nb * BLOCK)),
            scratch_shapes=[block16, block16, block16, natural, natural, pltpu.VMEM((nb, 8, BLOCK), f32), block32, block32, block32],
        ),
        compiler_params=pltpu.CompilerParams(dimension_semantics=("arbitrary",)),
        cost_estimate=pl.CostEstimate(
            flops=10 * heads * 20 * BLOCK * BLOCK * 256, bytes_accessed=8_000_000, transcendentals=heads * 20 * BLOCK * BLOCK
        ),
        name="attn_bwd",
    )(scal, *ops)


EPS = 1e-05
RING = 4


def turn(x, shift):
    return lax.ppermute(x, "tensor", [(i, (i + shift) % RING) for i in range(RING)])


def swap(x, axis, bit, size):
    return lax.ppermute(x, axis, [(i, i ^ bit) for i in range(size)])


def pick(x, index, axis=0):
    return lax.dynamic_index_in_dim(x, index, axis, keepdims=False)


def ring_gather(x):
    got = [x]
    for _ in range(RING - 1):
        got.append(turn(got[-1], 1))
    return got


def ring_reduce(chunks):
    moving = chunks[1].astype(bf16)
    for r in range(1, RING):
        moved = turn(moving, 1)
        total = moved.astype(f32) + chunks[(r + 1) % RING]
        moving = total.astype(bf16)
    return total


def spread_blocks(x, bits, size):
    for bit in bits:
        x = jnp.concatenate([x, swap(x, "dp", bit, size)])
    return x


def place_of(mask, bits):
    place = 0
    for k, bit in enumerate(bits):
        place = place + jnp.where(mask & bit != 0, 1 << k, 0)
    return place


def halve(blocks, left, bit, me, size):
    at = left.index(bit)
    lead, tail = 1 << at, 1 << (len(left) - at - 1)
    split = blocks.reshape((lead, 2, tail) + blocks.shape[1:])
    mine = jnp.where(me & bit != 0, 1, 0)
    send = pick(split, 1 - mine, 1).astype(bf16)
    keep = pick(split, mine, 1)
    total = keep.astype(f32) + swap(send, "dp", bit, size).astype(f32)
    return total.reshape((lead * tail,) + blocks.shape[1:]), [b for b in left if b != bit]


def centre(rows):
    shifted = rows - jnp.mean(rows, axis=-1, keepdims=True)
    rstd = lax.rsqrt(jnp.mean(shifted * shifted, axis=-1, keepdims=True) + EPS)
    return shifted * rstd, rstd


def norm_back(grad_hat, hat, rstd):
    return rstd * (
        grad_hat
        - jnp.mean(grad_hat, axis=-1, keepdims=True)
        - hat * jnp.mean(grad_hat * hat, axis=-1, keepdims=True)
    )


def gelu_both(v):
    inner = 0.7978845608028654 * (v + 0.044715 * v * v * v)
    t = jnp.tanh(inner)
    value = 0.5 * v * (1.0 + t)
    slope = 0.5 * (1.0 + t) + 0.5 * v * (1.0 - t * t) * 0.7978845608028654 * (1.0 + 3 * 0.044715 * v * v)
    return value, slope


def einf(spec, a, b):
    return jnp.einsum(spec, a, b, preferred_element_type=f32)


def shards(size, inputs, doc_ids, gain_attn, w_qkv, w_out, gain_mlp, w_up, w_down, grad_out):
    me = lax.axis_index("dp")
    z = lax.axis_index("tensor")
    odd = me & 1
    others = [1 << k for k in range(1, size.bit_length() - 1)]
    documents = doc_ids[0]
    tokens, dim = inputs.shape
    rows = dim // size
    hid = w_up.shape[1]
    half = hid // 2
    width = w_out.shape[0]
    scal = jnp.stack([z, jnp.sum(documents < 1), jnp.sum(documents < 2)]).astype(jnp.int32)

    pieces = [ring_gather(inputs[k : k + BLOCK]) for k in range(0, tokens, BLOCK)]

    gains = jnp.stack([gain_attn, gain_mlp])
    own = jnp.concatenate([w_qkv[0], w_qkv[1], w_qkv[2], jnp.pad(gains, ((0, 62), (0, 0))).T], axis=1)
    order = others + [1]
    spread_qkv = spread_blocks(own[None], order, size)
    full = jnp.concatenate([pick(spread_qkv, place_of(me ^ b, order)) for b in range(size)])
    full_qkv = full[:, : 3 * width]
    gain_one = full[:, 3 * width].astype(f32)
    gain_two = full[:, 3 * width + 1].astype(f32)

    out_rows = jnp.concatenate([w_out.T[: rows // 2], w_out.T[rows // 2 :]], axis=1)

    def pair_half(w):
        parts = w.reshape(rows, 2, half)
        return jnp.concatenate([pick(parts, odd, 1), swap(pick(parts, 1 - odd, 1), "dp", 1, size)])

    pack_a = jnp.concatenate([pair_half(w_up), out_rows])
    pack_b = pair_half(w_down.T)
    ring_a = jnp.stack(ring_gather(pack_a))
    ring_b = jnp.stack(ring_gather(pack_b))
    order_b = others[::-1]
    spread_a = spread_blocks(ring_a[None], others, size)
    spread_b = spread_blocks(ring_b[None], order_b, size)

    def assemble(spread_w, bits):
        blocks = []
        for b in range(size):
            mask = me ^ b
            block = pick(spread_w, place_of(mask, bits))[:, : 2 * rows]
            block = pick(block.reshape(RING, 2, rows, half), mask & 1, 1)
            blocks.append(block.transpose(1, 0, 2).reshape(rows, RING * half))
        return jnp.concatenate(blocks)

    full_up = assemble(spread_a, others)
    full_down = assemble(spread_b, order_b)
    out_part = spread_a[:, :, 2 * rows :]
    out_both = jnp.stack([out_part, swap(out_part, "dp", 1, size)])

    def out_block(b):
        mask = me ^ b
        block = pick(pick(out_both, mask & 1), place_of(mask, others))
        block = jnp.concatenate([block[..., :width], block[..., width:]], axis=1)
        return block.transpose(1, 0, 2).reshape(rows, RING * width)

    full_out = jnp.concatenate([out_block(b) for b in range(size)])
    grad_both = jnp.concatenate([grad_out, swap(grad_out, "dp", 1, size)])
    grad_active = einf("td,df->tf", grad_both, full_down)

    normed = []
    parts = []
    for s in range(RING):
        for piece in pieces:
            hat, _ = centre(piece[s].astype(f32))
            normed.append((hat * gain_one).astype(bf16))
            parts.append(einf("de,td->et", full_qkv, normed[-1]).astype(bf16))
    normed = jnp.concatenate(normed)
    sent, lse = attn_fwd(scal, parts)
    attended = jnp.concatenate([sent[0]] + [turn(sent[s], s) for s in range(1, RING)])
    mixed = inputs.astype(f32) + einf("et,de->td", attended, full_out)
    hat_two, rstd_two = centre(mixed)
    mlp_rows = (hat_two * gain_two).astype(bf16)
    mlp_both = jnp.concatenate([mlp_rows, swap(mlp_rows, "dp", 1, size)])
    hidden = einf("td,df->tf", mlp_both, full_up)
    value, slope = gelu_both(hidden)
    active = value.astype(bf16)
    grad_hidden = (grad_active * slope).astype(bf16)
    grad_part = einf("tf,df->td", grad_hidden, full_up)
    grad_mlp = grad_part[:tokens] + swap(grad_part[tokens:].astype(bf16), "dp", 1, size).astype(f32)
    grad_mixed = grad_out.astype(f32) + norm_back(grad_mlp * gain_two, hat_two, rstd_two)
    grad_branch = grad_mixed.astype(bf16)
    grad_att = einf("de,td->et", full_out, grad_branch).astype(bf16).reshape(RING, width, tokens)
    grads = [grad_att[0]] + [turn(grad_att[s], -s) for s in range(1, RING)]

    out_pair = einf("tf,df->td", active, full_down)
    layer_out = (
        mixed + out_pair[:tokens] + swap(out_pair[tokens:].astype(bf16), "dp", 1, size).astype(f32)
    ).astype(bf16)

    bits = [1 << k for k in reversed(range(size.bit_length() - 1))]

    def scatter(grad, stages, last_width):
        blocks, left = grad.reshape(size, rows, grad.shape[1]), list(bits)
        for bit in stages:
            blocks, left = halve(blocks, left, bit, me, size)
        blocks = blocks.reshape(-1, blocks.shape[-1])
        return ring_reduce([blocks[:, s * last_width : (s + 1) * last_width] for s in range(RING)])

    def pair_whole(block):
        block = block.reshape(2, rows, half)
        send = pick(block, 1 - odd).astype(bf16)
        keep = pick(block, odd)
        other = swap(send, "dp", 1, size).astype(f32)
        return jnp.where(odd == 0, jnp.concatenate([keep, other], axis=1), jnp.concatenate([other, keep], axis=1))

    grad_down = pair_whole(scatter(einf("td,tf->df", grad_both, active), others, half)).T
    grad_up = pair_whole(scatter(einf("td,tf->df", mlp_both, grad_hidden), order_b, half))
    grad_o = scatter(einf("td,et->de", grad_branch, attended), [1] + order_b, width).T

    grad_parts = attn_bwd(scal, parts, sent, grads, lse)
    grad_proj = einf("td,et->de", normed, grad_parts)
    blocks, left = grad_proj.reshape(size, rows, 3 * width), list(bits)
    for bit in [1] + order_b:
        blocks, left = halve(blocks, left, bit, me, size)
    grad_qkv = blocks[0].reshape(rows, 3, width).transpose(1, 0, 2)

    back = []
    for k in range(0, tokens, BLOCK):
        back.append(
            ring_reduce(
                [
                    einf("et,de->td", grad_parts[:, s * tokens + k : s * tokens + k + BLOCK], full_qkv)
                    for s in range(RING)
                ]
            )
        )
    grad_normed = jnp.concatenate(back)
    hat_one, rstd_one = centre(inputs.astype(f32))
    grad_inputs = grad_mixed + norm_back(grad_normed * gain_one, hat_one, rstd_one)

    sums = jnp.stack(
        [
            jnp.sum(w_qkv.astype(f32) * grad_qkv, axis=(0, 2)),
            jnp.sum(w_up.astype(f32) * grad_up, axis=1),
        ]
    )
    for bit in (1, 2):
        sums = sums + swap(sums, "tensor", bit, RING)
    sums = sums / gains.astype(f32)
    return layer_out, grad_inputs, sums[0], grad_qkv, grad_o, sums[1], grad_up, grad_down


def solution(mesh):
    both = P(("dp", "tensor"), None)
    weights = (P(None, "dp", "tensor"), P("tensor", "dp"), P("dp"), P("dp", "tensor"), P("tensor", "dp"))
    return jax.shard_map(
        functools.partial(shards, mesh.shape["dp"]),
        mesh=mesh,
        in_specs=(both, P("dp", None), P("dp"), *weights, both),
        out_specs=(both, both, P("dp"), *weights),
        check_vma=False,
    )
```

time: 1010 us -> 383 us (0.38)
  waiting for transfers between devices: 633 us -> 98 us
  matrix products: 193 us -> 65.4 us
  blocking collectives: 61.4 us -> 0 us
  starting transfers between devices: 1.76 us -> 60.2 us
  Pallas kernels: 0 us -> 45.6 us
  local copies, waits for them, and re-layouts: 28.4 us -> 56.6 us
  other arithmetic: 71.2 us -> 47 us
  between operations: 19.7 us -> 2.92 us
    reduce_scatter x6 -> x0, waiting for transfers between devices: 422 us -> none  [the longest x1 141 us: shards(): lax.psum_scatter(jnp.dot(attended, full_out, preferred_element_type=jnp.f...]
    all_gather x6 -> x0, waiting for transfers between devices: 195 us -> none  [the longest x1 65.5 us: shards(): mlp_all = lax.all_gather(mlp_rows, 'tensor', axis=0, tiled=True)]
    dot_general x82 -> x26, matrix products: 187 us -> 65.4 us  [einf(): return jnp.einsum(spec, a, b, preferred_element_type=f32)]
    ppermute x0 -> x61, waiting for transfers between devices: none -> 98 us  [the longest x33 80.5 us: turn(): lax.ppermute(x, 'tensor', [(i, (i + shift) % RING) for i in range(RING)])]
    ppermute x0 -> x61, starting transfers between devices: none -> 60.2 us  [the longest x33 31.4 us: turn(): lax.ppermute(x, 'tensor', [(i, (i + shift) % RING) for i in range(RING)])]
    pallas_call x0 -> x2, Pallas kernels: none -> 45.7 us  [the longest x1 23.9 us: attn_bwd(): pl.pallas_call(attn_bwd_body, out_shape=jax.ShapeDtypeStruct((3 * width,...]
    convert_element_type x11 -> x10, other arithmetic: 38.8 us -> 0.76 us  [the longest x1 0.3 us: shards(): gain_two = full[:, 3 * width + 1].astype(f32)]
    unnamed x2 -> x0, blocking collectives: 29.1 us -> none
  transfers between devices with their start and end apart: 14 -> 61, of which waited for: 12 -> 27; matrix products, arithmetic and copies ran while one was open for 17% -> 34% of each run, Pallas kernels for 0% -> 12%
where the time goes in v1:
time: 383 us; the launch traced here: 376 us
  waiting for transfers between devices  98 us (26%)
  matrix products  65.4 us (17%)
  starting transfers between devices  60.2 us (16%)
  local copies, waits for them, and re-layouts  56.6 us (15%)
  other arithmetic  47 us (12%)
  Pallas kernels  45.6 us (12%)
    ppermute x33, waiting for transfers between devices, turn(): lax.ppermute(x, 'tensor', [(i, (i + shift) % RING) for i in range(RING)])  80.5 us
    dot_general x26, matrix products, einf(): return jnp.einsum(spec, a, b, preferred_element_type=f32)  65.4 us
    ppermute x33, starting transfers between devices, turn(): lax.ppermute(x, 'tensor', [(i, (i + shift) % RING) for i in range(RING)])  31.4 us
    ppermute x28, starting transfers between devices, swap(): return lax.ppermute(x, axis, [(i, i ^ bit) for i in range(size)])  28.9 us
    pallas_call x1, Pallas kernels, attn_bwd(): pl.pallas_call(attn_bwd_body, out_shape=jax.ShapeDtypeStruct((3 * width,...  23.9 us
    pallas_call x1, Pallas kernels, attn_fwd(): pl.pallas_call(attn_fwd_body, out_shape=(jax.ShapeDtypeStruct((4, width,...  21.7 us
    unnamed x162, local copies, waits for them, and re-layouts  19.4 us
    ppermute x28, waiting for transfers between devices, swap(): return lax.ppermute(x, axis, [(i, i ^ bit) for i in range(size)])  17.4 us
  transfers between devices with their start and end apart: 61, of which 27 were waited for; matrix products, arithmetic and copies ran while one was open for 34% of the time, Pallas kernels for 12%

profile of v1, /device:TPU:0, one launch (start us, length us, event | category | flops | bytes accessed | tf_op | source)
XLA Modules:
  0.0 375.7 jit_solution(18154801848820958502)
XLA Ops:
  2.5 3.0 collective-permute-start
  16.3 2.7 collective-permute-done.21
  26.3 5.4 %collective-permute-done.14 = bf16[240,384]{1,0:T(8,128)(2,1)S(1)} collective-permute-done((bf16[240,384]{1,0:T(8,128)(2,1)S(1)}, bf16[240,384]{1,0:T(8,128)(2,1)S(1)}, u32[]{:S(2)}, u32[]{:S(2)}) %collective-permute-start.14) | collective-permute-done | bytes 184352 | tf_op jit(solution)/shard_map/ppermute | solution.py:222
  36.3 2.8 collective-permute-done.15
  50.9 6.8 %collective-permute-done.4 = bf16[256,768]{1,0:T(8,128)(2,1)S(1)} collective-permute-done((bf16[256,768]{1,0:T(8,128)(2,1)S(1)}, bf16[256,768]{1,0:T(8,128)(2,1)S(1)}, u32[]{:S(2)}, u32[]{:S(2)}) %collective-permute-start.4) | collective-permute-done | bytes 393248 | tf_op jit(solution)/shard_map/ppermute | solution.py:222
  57.9 4.1 %collective-permute-done.3 = bf16[256,768]{1,0:T(8,128)(2,1)S(1)} collective-permute-done((bf16[256,768]{1,0:T(8,128)(2,1)S(1)}, bf16[256,768]{1,0:T(8,128)(2,1)S(1)}, u32[]{:S(2)}, u32[]{:S(2)}) %collective-permute-start.3) | collective-permute-done | bytes 393248 | tf_op jit(solution)/shard_map/ppermute | solution.py:222
  68.3 6.8 %collective-permute-done.6 = bf16[256,768]{1,0:T(8,128)(2,1)S(1)} collective-permute-done((bf16[256,768]{1,0:T(8,128)(2,1)S(1)}, bf16[256,768]{1,0:T(8,128)(2,1)S(1)}, u32[]{:S(2)}, u32[]{:S(2)}) %collective-permute-start.6) | collective-permute-done | bytes 393248 | tf_op jit(solution)/shard_map/ppermute | solution.py:222
  75.4 4.2 %collective-permute-done.5 = bf16[256,768]{1,0:T(8,128)(2,1)S(1)} collective-permute-done((bf16[256,768]{1,0:T(8,128)(2,1)S(1)}, bf16[256,768]{1,0:T(8,128)(2,1)S(1)}, u32[]{:S(2)}, u32[]{:S(2)}) %collective-permute-start.5) | collective-permute-done | bytes 393248 | tf_op jit(solution)/shard_map/ppermute | solution.py:222
  84.0 7.9 %collective-permute-done.8 = bf16[256,768]{1,0:T(8,128)(2,1)S(1)} collective-permute-done((bf16[256,768]{1,0:T(8,128)(2,1)S(1)}, bf16[256,768]{1,0:T(8,128)(2,1)S(1)}, u32[]{:S(2)}, u32[]{:S(2)}) %collective-permute-start.8) | collective-permute-done | bytes 393248 | tf_op jit(solution)/shard_map/ppermute | solution.py:222
  92.3 3.8 %collective-permute-done.7 = bf16[256,768]{1,0:T(8,128)(2,1)S(1)} collective-permute-done((bf16[256,768]{1,0:T(8,128)(2,1)S(1)}, bf16[256,768]{1,0:T(8,128)(2,1)S(1)}, u32[]{:S(2)}, u32[]{:S(2)}) %collective-permute-start.7) | collective-permute-done | bytes 393248 | tf_op jit(solution)/shard_map/ppermute | solution.py:222
  99.1 21.7 %attn_fwd.1 = (bf16[4,192,512]{2,1,0:T(8,128)(2,1)}, f32[8,8,256]{2,1,0:T(8,128)}) custom-call(s32[3]{0:T(128)} %pad_add_fusion.scal, bf16[576,256]{1,0:T(8,128)(2,1)} %convolution_convert_fusion.10.refs_0_, bf16[576,256]{1,0:T(8,128)(2,1)} %convolution_convert_fusion.9.refs_1_, bf16[576,256]{1,0:T(8,128)(2,1)} %convolution_convert_fusion.8.refs_2_, ...), custom_call_target="tpu_custom_call" | custom-call | flops 4026531840 | bytes 4000000 | tf_op jit(solution)/shard_map/attn_fwd/pallas_call | solution.py:104
  161.1 2.6 fusion.22
  163.7 14.0 %fusion.159 = f32[1024,768]{1,0:T(8,128)S(1)} fusion(bf16[768,1536]{1,0:T(8,128)(2,1)S(1)} %copy-done.45, f32[1024,1536]{1,0:T(8,128)S(1)} %fusion.22), kind=kOutput, calls=%fused_computation.393 | convolution fusion | flops 2430074880 | bytes 11796480 | tf_op jit(solution)/shard_map/tf,df->td/dot_general | solution.py:296
  177.7 5.9 %fusion.6 = bf16[1024,1536]{1,0:T(8,128)(2,1)S(1)} fusion(f32[1024,1536]{1,0:T(8,128)S(1)} %fusion.22, bf16[1024,768]{1,0:T(8,128)(2,1)S(1)} %copy-done.36, bf16[768,1536]{1,0:T(8,128)(2,1)S(1)} %copy-done.45), kind=kOutput, calls=%fused_computation.8 | convolution fusion | flops 2445803520 | bytes 13369344 | tf_op jit(solution)/shard_map/td,df->tf/dot_general | solution.py:296
  183.6 2.9 fusion.158
  186.5 2.6 fusion.171
  189.9 2.6 fusion.21
  193.9 2.6 collective-permute-start.41
  197.6 4.4 %collective-permute-start.55 = (bf16[2,2,96,1536]{3,2,1,0:T(8,128)(2,1)}, bf16[2,2,96,1536]{3,2,1,0:T(8,128)(2,1)}, u32[]{:S(2)}, u32[]{:S(2)}) collective-permute-start(bf16[2,2,96,1536]{3,2,1,0:T(8,128)(2,1)} %fusion.20), channel_id=1, source_target_pairs={{0,8},{4,12},{8,0},{12,4},{16,24},{20,28},{24,16},{28,20},{1,9},{5... | collective-permute-start | bytes 3538952 | tf_op jit(solution)/shard_map/ppermute | solution.py:226
  208.8 3.1 collective-permute-start.29
  216.1 7.0 %collective-permute-done.30.refs_11_ = bf16[192,512]{1,0:T(8,128)(2,1)S(1)} collective-permute-done((bf16[192,512]{1,0:T(8,128)(2,1)S(1)}, bf16[192,512]{1,0:T(8,128)(2,1)S(1)}, u32[]{:S(2)}, u32[]{:S(2)}) %collective-permute-start.30) | collective-permute-done | bytes 196640 | tf_op jit(solution)/shard_map/ppermute | solution.py:222
  223.9 23.9 %attn_bwd.1 = bf16[576,2048]{1,0:T(8,128)(2,1)} custom-call(s32[3]{0:T(128)} %pad_add_fusion.scal, bf16[576,256]{1,0:T(8,128)(2,1)} %convolution_convert_fusion.10.refs_0_, bf16[576,256]{1,0:T(8,128)(2,1)} %convolution_convert_fusion.9.refs_1_, bf16[576,256]{1,0:T(8,128)(2,1)} %convolution_convert_fusion.8.refs_2_, ...), custom_call_target="tpu_custom_call" | custom-call | flops 10066329600 | bytes 8000000 | tf_op jit(solution)/shard_map/attn_bwd/pallas_call | solution.py:199
  250.3 4.6 %collective-permute-start.32 = (bf16[256,768]{1,0:T(8,128)(2,1)}, bf16[256,768]{1,0:T(8,128)(2,1)}, u32[]{:S(2)}, u32[]{:S(2)}) collective-permute-start(bf16[256,768]{1,0:T(8,128)(2,1)} %convolution_convert_fusion.2), channel_id=1, source_target_pairs={{0,1},{1,2},{2,3},{3,0},{4,5},{5,6},{6,7},{7,4},{8,9},{9,10},{10,1... | collective-permute-start | bytes 1179656 | tf_op jit(solution)/shard_map/ppermute | solution.py:222
  254.8 5.3 %fusion.172 = f32[768,576]{1,0:T(8,128)S(1)} fusion(bf16[2048,768]{1,0:T(8,128)(2,1)} %constant_dynamic-update-slice_fusion.26, bf16[576,2048]{1,0:T(8,128)(2,1)} %attn_bwd.1), kind=kOutput, calls=%fused_computation.406 | convolution fusion | flops 1811939328 | bytes 7274496 | tf_op jit(solution)/shard_map/td,et->de/dot_general | solution.py:296
  268.2 4.9 %collective-permute-start.42 = (bf16[1,2,96,1536]{3,2,1,0:T(8,128)(2,1)}, bf16[1,2,96,1536]{3,2,1,0:T(8,128)(2,1)}, u32[]{:S(2)}, u32[]{:S(2)}) collective-permute-start(bf16[1,2,96,1536]{3,2,1,0:T(8,128)(2,1)} %fusion.64), channel_id=1, source_target_pairs={{0,8},{4,12},{8,0},{12,4},{16,24},{20,28},{24,16},{28,20},{1,9},{5... | collective-permute-start | bytes 1769480 | tf_op jit(solution)/shard_map/ppermute | solution.py:226
  280.4 2.9 copy.82
  301.1 6.4 %collective-permute-done.39 = bf16[1,2,96,576]{2,3,1,0:T(8,128)(2,1)} collective-permute-done((bf16[1,2,96,576]{2,3,1,0:T(8,128)(2,1)}, bf16[1,2,96,576]{2,3,1,0:T(8,128)(2,1)}, u32[]{:S(2)}, u32[]{:S(2)}) %collective-permute-start.39) | collective-permute-done | bytes 221216 | tf_op jit(solution)/shard_map/ppermute | solution.py:226
  328.9 2.5 collective-permute-start.34
  335.8 8.2 %collective-permute-done.53 = bf16[96,192]{0,1:T(8,128)(2,1)S(1)} collective-permute-done((bf16[96,192]{0,1:T(8,128)(2,1)S(1)}, bf16[96,192]{0,1:T(8,128)(2,1)S(1)}, u32[]{:S(2)}, u32[]{:S(2)}) %collective-permute-start.53) | collective-permute-done | bytes 36896 | tf_op jit(solution)/shard_map/ppermute | solution.py:222
  347.0 6.5 %collective-permute-done.54 = bf16[96,192]{0,1:T(8,128)(2,1)S(1)} collective-permute-done((bf16[96,192]{0,1:T(8,128)(2,1)S(1)}, bf16[96,192]{0,1:T(8,128)(2,1)S(1)}, u32[]{:S(2)}, u32[]{:S(2)}) %collective-permute-start.54) | collective-permute-done | bytes 36896 | tf_op jit(solution)/shard_map/ppermute | solution.py:222
  366.9 3.3 collective-permute-done.47
  372.0 2.7 collective-permute-done.48
  (475 shorter events, 184.6 us)
Async XLA Ops:
  8.8 31.9 %collective-permute-start.27 = (bf16[512,768]{1,0:T(8,128)(2,1)S(1)}, bf16[512,768]{1,0:T(8,128)(2,1)}, u32[]{:S(2)}, u32[]{:S(2)}) collective-permute-start(bf16[512,768]{1,0:T(8,128)(2,1)S(1)} %copy-done.8), channel_id=1, source_target_pairs={{0,4},{4,0},{8,12},{12,8},{16,20},{20,16},{24,28},{28,24},{1,5},{5... | collective-permute-start | bytes 2359304 | tf_op jit(solution)/shard_map/ppermute | solution.py:226
  26.3 16.8 %collective-permute-start.2 = (bf16[4,96,640]{2,1,0:T(8,128)(2,1)S(1)}, bf16[4,96,640]{2,1,0:T(8,128)(2,1)S(1)}, u32[]{:S(2)}, u32[]{:S(2)}) collective-permute-start(bf16[4,96,640]{2,1,0:T(8,128)(2,1)S(1)} %pad_maximum_fusion.9), channel_id=1, source_target_pairs={{0,4},{4,0},{8,12},{12,8},{16,20},{20,16},{24,28},{28,24},{1,5},{5... | collective-permute-start | bytes 1474568 | tf_op jit(solution)/shard_map/ppermute | solution.py:226
  34.7 14.1 %collective-permute-start.24 = (bf16[1,4,192,384]{3,2,1,0:T(8,128)(2,1)S(1)}, bf16[1,4,192,384]{3,2,1,0:T(8,128)(2,1)S(1)}, u32[]{:S(2)}, u32[]{:S(2)}) collective-permute-start(bf16[1,4,192,384]{3,2,1,0:T(8,128)(2,1)S(1)} %maximum_bitcast_fusion.1), channel_id=1, source_target_pairs={{0,16},{4,20},{8,24},{12,28},{16,0},{20,4},{24,8},{28,12},{1,17},{... | collective-permute-start | bytes 1769480 | tf_op jit(solution)/shard_map/ppermute | solution.py:226
  40.1 25.6 %collective-permute-start.16 = (bf16[1,4,240,384]{3,2,1,0:T(8,128)(2,1)S(1)}, bf16[1,4,240,384]{3,2,1,0:T(8,128)(2,1)S(1)}, u32[]{:S(2)}, u32[]{:S(2)}) collective-permute-start(bf16[1,4,240,384]{3,2,1,0:T(8,128)(2,1)S(1)} %maximum_bitcast_fusion), channel_id=1, source_target_pairs={{0,8},{4,12},{8,0},{12,4},{16,24},{20,28},{24,16},{28,20},{1,9},{5... | collective-permute-start | bytes 2211848 | tf_op jit(solution)/shard_map/ppermute | solution.py:226
  44.2 13.5 %collective-permute-start.4 = (bf16[256,768]{1,0:T(8,128)(2,1)S(1)}, bf16[256,768]{1,0:T(8,128)(2,1)S(1)}, u32[]{:S(2)}, u32[]{:S(2)}) collective-permute-start(bf16[256,768]{1,0:T(8,128)(2,1)S(1)} %get-tuple-element.77), channel_id=1, source_target_pairs={{0,1},{1,2},{2,3},{3,0},{4,5},{5,6},{6,7},{7,4},{8,9},{9,10},{10,1... | collective-permute-start | bytes 1179656 | tf_op jit(solution)/shard_map/ppermute | solution.py:222
  44.3 17.7 %collective-permute-start.3 = (bf16[256,768]{1,0:T(8,128)(2,1)S(1)}, bf16[256,768]{1,0:T(8,128)(2,1)S(1)}, u32[]{:S(2)}, u32[]{:S(2)}) collective-permute-start(bf16[256,768]{1,0:T(8,128)(2,1)S(1)} %get-tuple-element.78), channel_id=1, source_target_pairs={{0,1},{1,2},{2,3},{3,0},{4,5},{5,6},{6,7},{7,4},{8,9},{9,10},{10,1... | collective-permute-start | bytes 1179656 | tf_op jit(solution)/shard_map/ppermute | solution.py:222
  50.0 78.0 %collective-permute-start.25 = (bf16[2,4,192,384]{3,2,1,0:T(8,128)(2,1)}, bf16[2,4,192,384]{3,2,1,0:T(8,128)(2,1)}, u32[]{:S(2)}, u32[]{:S(2)}) collective-permute-start(bf16[2,4,192,384]{3,2,1,0:T(8,128)(2,1)} %pad_maximum_fusion.4), channel_id=1, source_target_pairs={{0,8},{4,12},{8,0},{12,4},{16,24},{20,28},{24,16},{28,20},{1,9},{5... | collective-permute-start | bytes 3538952 | tf_op jit(solution)/shard_map/ppermute | solution.py:226
  62.4 17.2 %collective-permute-start.5 = (bf16[256,768]{1,0:T(8,128)(2,1)S(1)}, bf16[256,768]{1,0:T(8,128)(2,1)S(1)}, u32[]{:S(2)}, u32[]{:S(2)}) collective-permute-start(bf16[256,768]{1,0:T(8,128)(2,1)S(1)} %collective-permute-done.3), channel_id=1, source_target_pairs={{0,1},{1,2},{2,3},{3,0},{4,5},{5,6},{6,7},{7,4},{8,9},{9,10},{10,1... | collective-permute-start | bytes 1179656 | tf_op jit(solution)/shard_map/ppermute | solution.py:222
  67.2 63.1 %collective-permute-start.17 = (bf16[2,4,240,384]{3,2,1,0:T(8,128)(2,1)}, bf16[2,4,240,384]{3,2,1,0:T(8,128)(2,1)}, u32[]{:S(2)}, u32[]{:S(2)}) collective-permute-start(bf16[2,4,240,384]{3,2,1,0:T(8,128)(2,1)} %pad_maximum_fusion.3), channel_id=1, source_target_pairs={{0,16},{4,20},{8,24},{12,28},{16,0},{20,4},{24,8},{28,12},{1,17},{... | collective-permute-start | bytes 4423688 | tf_op jit(solution)/shard_map/ppermute | solution.py:226
  80.1 16.0 %collective-permute-start.7 = (bf16[256,768]{1,0:T(8,128)(2,1)S(1)}, bf16[256,768]{1,0:T(8,128)(2,1)S(1)}, u32[]{:S(2)}, u32[]{:S(2)}) collective-permute-start(bf16[256,768]{1,0:T(8,128)(2,1)S(1)} %collective-permute-done.5), channel_id=1, source_target_pairs={{0,1},{1,2},{2,3},{3,0},{4,5},{5,6},{6,7},{7,4},{8,9},{9,10},{10,1... | collective-permute-start | bytes 1179656 | tf_op jit(solution)/shard_map/ppermute | solution.py:222
  123.0 33.0 %collective-permute-start.11 = (bf16[192,512]{1,0:T(8,128)(2,1)}, bf16[192,512]{1,0:T(8,128)(2,1)}, u32[]{:S(2)}, u32[]{:S(2)}) collective-permute-start(bf16[192,512]{1,0:T(8,128)(2,1)} %get-tuple-element.84), channel_id=1, source_target_pairs={{0,3},{1,0},{2,1},{3,2},{4,7},{5,4},{6,5},{7,6},{8,11},{9,8},{10,9... | collective-permute-start | bytes 589832 | tf_op jit(solution)/shard_map/ppermute | solution.py:222
  123.0 32.9 %collective-permute-start.10 = (bf16[192,512]{1,0:T(8,128)(2,1)}, bf16[192,512]{1,0:T(8,128)(2,1)}, u32[]{:S(2)}, u32[]{:S(2)}) collective-permute-start(bf16[192,512]{1,0:T(8,128)(2,1)} %get-tuple-element.85), channel_id=1, source_target_pairs={{0,2},{1,3},{2,0},{3,1},{4,6},{5,7},{6,4},{7,5},{8,10},{9,11},{10,... | collective-permute-start | bytes 589832 | tf_op jit(solution)/shard_map/ppermute | solution.py:222
  123.1 32.9 %collective-permute-start.9 = (bf16[192,512]{1,0:T(8,128)(2,1)}, bf16[192,512]{1,0:T(8,128)(2,1)}, u32[]{:S(2)}, u32[]{:S(2)}) collective-permute-start(bf16[192,512]{1,0:T(8,128)(2,1)} %get-tuple-element.86), channel_id=1, source_target_pairs={{0,1},{1,2},{2,3},{3,0},{4,5},{5,6},{6,7},{7,4},{8,9},{9,10},{10,1... | collective-permute-start | bytes 589832 | tf_op jit(solution)/shard_map/ppermute | solution.py:222
  189.8 12.8 %collective-permute-start.26 = (bf16[512,768]{1,0:T(8,128)(2,1)S(1)}, bf16[512,768]{1,0:T(8,128)(2,1)S(1)}, u32[]{:S(2)}, u32[]{:S(2)}) collective-permute-start(bf16[512,768]{1,0:T(8,128)(2,1)S(1)} %slice.472), channel_id=1, source_target_pairs={{0,4},{4,0},{8,12},{12,8},{16,20},{20,16},{24,28},{28,24},{1,5},{5... | collective-permute-start | bytes 2359304 | tf_op jit(solution)/shard_map/ppermute | solution.py:226
  193.9 69.8 %collective-permute-start.41 = (bf16[1,4,96,1536]{3,2,1,0:T(8,128)(2,1)}, bf16[1,4,96,1536]{3,2,1,0:T(8,128)(2,1)}, u32[]{:S(2)}, u32[]{:S(2)}) collective-permute-start(bf16[1,4,96,1536]{3,2,1,0:T(8,128)(2,1)} %fusion.19), channel_id=1, source_target_pairs={{0,16},{4,20},{8,24},{12,28},{16,0},{20,4},{24,8},{28,12},{1,17},{... | collective-permute-start | bytes 3538952 | tf_op jit(solution)/shard_map/ppermute | solution.py:226
  197.6 70.6 %collective-permute-start.55 = (bf16[2,2,96,1536]{3,2,1,0:T(8,128)(2,1)}, bf16[2,2,96,1536]{3,2,1,0:T(8,128)(2,1)}, u32[]{:S(2)}, u32[]{:S(2)}) collective-permute-start(bf16[2,2,96,1536]{3,2,1,0:T(8,128)(2,1)} %fusion.20), channel_id=1, source_target_pairs={{0,8},{4,12},{8,0},{12,4},{16,24},{20,28},{24,16},{28,20},{1,9},{5... | collective-permute-start | bytes 3538952 | tf_op jit(solution)/shard_map/ppermute | solution.py:226
  207.8 15.3 %collective-permute-start.30 = (bf16[192,512]{1,0:T(8,128)(2,1)S(1)}, bf16[192,512]{1,0:T(8,128)(2,1)S(1)}, u32[]{:S(2)}, u32[]{:S(2)}) collective-permute-start(bf16[192,512]{1,0:T(8,128)(2,1)S(1)} %get-tuple-element.80), channel_id=1, source_target_pairs={{0,2},{1,3},{2,0},{3,1},{4,6},{5,7},{6,4},{7,5},{8,10},{9,11},{10,... | collective-permute-start | bytes 589832 | tf_op jit(solution)/shard_map/ppermute | solution.py:222
  208.8 14.3 %collective-permute-start.29 = (bf16[192,512]{1,0:T(8,128)(2,1)S(1)}, bf16[192,512]{1,0:T(8,128)(2,1)S(1)}, u32[]{:S(2)}, u32[]{:S(2)}) collective-permute-start(bf16[192,512]{1,0:T(8,128)(2,1)S(1)} %get-tuple-element.81), channel_id=1, source_target_pairs={{0,3},{1,0},{2,1},{3,2},{4,7},{5,4},{6,5},{7,6},{8,11},{9,8},{10,9... | collective-permute-start | bytes 589832 | tf_op jit(solution)/shard_map/ppermute | solution.py:222
  216.1 60.9 %collective-permute-start.49 = (bf16[4,1,96,768]{3,2,0,1:T(8,128)(2,1)}, bf16[4,1,96,768]{3,2,0,1:T(8,128)(2,1)}, u32[]{:S(2)}, u32[]{:S(2)}) collective-permute-start(bf16[4,1,96,768]{3,2,0,1:T(8,128)(2,1)} %fusion.65), channel_id=1, source_target_pairs={{0,4},{4,0},{8,12},{12,8},{16,20},{20,16},{24,28},{28,24},{1,5},{5... | collective-permute-start | bytes 1769480 | tf_op jit(solution)/shard_map/ppermute | solution.py:226
  250.3 35.1 %collective-permute-start.32 = (bf16[256,768]{1,0:T(8,128)(2,1)}, bf16[256,768]{1,0:T(8,128)(2,1)}, u32[]{:S(2)}, u32[]{:S(2)}) collective-permute-start(bf16[256,768]{1,0:T(8,128)(2,1)} %convolution_convert_fusion.2), channel_id=1, source_target_pairs={{0,1},{1,2},{2,3},{3,0},{4,5},{5,6},{6,7},{7,4},{8,9},{9,10},{10,1... | collective-permute-start | bytes 1179656 | tf_op jit(solution)/shard_map/ppermute | solution.py:222
  262.6 33.1 %collective-permute-start.35 = (bf16[256,768]{1,0:T(8,128)(2,1)}, bf16[256,768]{1,0:T(8,128)(2,1)}, u32[]{:S(2)}, u32[]{:S(2)}) collective-permute-start(bf16[256,768]{1,0:T(8,128)(2,1)} %convolution_convert_fusion.1), channel_id=1, source_target_pairs={{0,1},{1,2},{2,3},{3,0},{4,5},{5,6},{6,7},{7,4},{8,9},{9,10},{10,1... | collective-permute-start | bytes 1179656 | tf_op jit(solution)/shard_map/ppermute | solution.py:222
  263.7 25.0 %collective-permute-start.38 = (bf16[4,1,96,576]{3,2,0,1:T(8,128)(2,1)}, bf16[4,1,96,576]{3,2,0,1:T(8,128)(2,1)}, u32[]{:S(2)}, u32[]{:S(2)}) collective-permute-start(bf16[4,1,96,576]{3,2,0,1:T(8,128)(2,1)} %fusion.66), channel_id=1, source_target_pairs={{0,4},{4,0},{8,12},{12,8},{16,20},{20,16},{24,28},{28,24},{1,5},{5... | collective-permute-start | bytes 1327112 | tf_op jit(solution)/shard_map/ppermute | solution.py:226
  268.2 52.4 %collective-permute-start.42 = (bf16[1,2,96,1536]{3,2,1,0:T(8,128)(2,1)}, bf16[1,2,96,1536]{3,2,1,0:T(8,128)(2,1)}, u32[]{:S(2)}, u32[]{:S(2)}) collective-permute-start(bf16[1,2,96,1536]{3,2,1,0:T(8,128)(2,1)} %fusion.64), channel_id=1, source_target_pairs={{0,8},{4,12},{8,0},{12,4},{16,24},{20,28},{24,16},{28,20},{1,9},{5... | collective-permute-start | bytes 1769480 | tf_op jit(solution)/shard_map/ppermute | solution.py:226
  277.0 45.5 %collective-permute-start.56 = (bf16[1,2,96,1536]{3,2,1,0:T(8,128)(2,1)}, bf16[1,2,96,1536]{3,2,1,0:T(8,128)(2,1)}, u32[]{:S(2)}, u32[]{:S(2)}) collective-permute-start(bf16[1,2,96,1536]{3,2,1,0:T(8,128)(2,1)} %dynamic-slice_convert_fusion.2), channel_id=1, source_target_pairs={{0,16},{4,20},{8,24},{12,28},{16,0},{20,4},{24,8},{28,12},{1,17},{... | collective-permute-start | bytes 1769480 | tf_op jit(solution)/shard_map/ppermute | solution.py:226
  285.3 25.8 %collective-permute-start.50 = (bf16[1,2,96,768]{2,3,1,0:T(8,128)(2,1)}, bf16[1,2,96,768]{2,3,1,0:T(8,128)(2,1)}, u32[]{:S(2)}, u32[]{:S(2)}) collective-permute-start(bf16[1,2,96,768]{2,3,1,0:T(8,128)(2,1)} %fusion.67), channel_id=1, source_target_pairs={{0,16},{4,20},{8,24},{12,28},{16,0},{20,4},{24,8},{28,12},{1,17},{... | collective-permute-start | bytes 884744 | tf_op jit(solution)/shard_map/ppermute | solution.py:226
  288.7 38.7 %collective-permute-start.33 = (bf16[256,768]{1,0:T(8,128)(2,1)}, bf16[256,768]{1,0:T(8,128)(2,1)}, u32[]{:S(2)}, u32[]{:S(2)}) collective-permute-start(bf16[256,768]{1,0:T(8,128)(2,1)} %add_convert_fusion.3), channel_id=1, source_target_pairs={{0,1},{1,2},{2,3},{3,0},{4,5},{5,6},{6,7},{7,4},{8,9},{9,10},{10,1... | collective-permute-start | bytes 1179656 | tf_op jit(solution)/shard_map/ppermute | solution.py:222
  307.5 26.2 %collective-permute-start.36 = (bf16[256,768]{1,0:T(8,128)(2,1)}, bf16[256,768]{1,0:T(8,128)(2,1)}, u32[]{:S(2)}, u32[]{:S(2)}) collective-permute-start(bf16[256,768]{1,0:T(8,128)(2,1)} %add_convert_fusion.1), channel_id=1, source_target_pairs={{0,1},{1,2},{2,3},{3,0},{4,5},{5,6},{6,7},{7,4},{8,9},{9,10},{10,1... | collective-permute-start | bytes 1179656 | tf_op jit(solution)/shard_map/ppermute | solution.py:222
  322.2 22.3 %collective-permute-start.43 = (bf16[192,384]{1,0:T(8,128)(2,1)S(1)}, bf16[192,384]{1,0:T(8,128)(2,1)S(1)}, u32[]{:S(2)}, u32[]{:S(2)}) collective-permute-start(bf16[192,384]{1,0:T(8,128)(2,1)S(1)} %slice.474), channel_id=1, source_target_pairs={{0,1},{1,2},{2,3},{3,0},{4,5},{5,6},{6,7},{7,4},{8,9},{9,10},{10,1... | collective-permute-start | bytes 442376 | tf_op jit(solution)/shard_map/ppermute | solution.py:222
  324.0 21.1 %collective-permute-start.57 = (bf16[192,384]{1,0:T(8,128)(2,1)S(1)}, bf16[192,384]{1,0:T(8,128)(2,1)S(1)}, u32[]{:S(2)}, u32[]{:S(2)}) collective-permute-start(bf16[192,384]{1,0:T(8,128)(2,1)S(1)} %slice.473), channel_id=1, source_target_pairs={{0,1},{1,2},{2,3},{3,0},{4,5},{5,6},{6,7},{7,4},{8,9},{9,10},{10,1... | collective-permute-start | bytes 442376 | tf_op jit(solution)/shard_map/ppermute | solution.py:222
  328.9 30.2 %collective-permute-start.34 = (bf16[256,768]{1,0:T(8,128)(2,1)S(1)}, bf16[256,768]{1,0:T(8,128)(2,1)S(1)}, u32[]{:S(2)}, u32[]{:S(2)}) collective-permute-start(bf16[256,768]{1,0:T(8,128)(2,1)S(1)} %add_convert_fusion.2), channel_id=1, source_target_pairs={{0,1},{1,2},{2,3},{3,0},{4,5},{5,6},{6,7},{7,4},{8,9},{9,10},{10,1... | collective-permute-start | bytes 1179656 | tf_op jit(solution)/shard_map/ppermute | solution.py:222
  335.3 24.4 %collective-permute-start.37 = (bf16[256,768]{1,0:T(8,128)(2,1)S(1)}, bf16[256,768]{1,0:T(8,128)(2,1)S(1)}, u32[]{:S(2)}, u32[]{:S(2)}) collective-permute-start(bf16[256,768]{1,0:T(8,128)(2,1)S(1)} %add_convert_fusion), channel_id=1, source_target_pairs={{0,1},{1,2},{2,3},{3,0},{4,5},{5,6},{6,7},{7,4},{8,9},{9,10},{10,1... | collective-permute-start | bytes 1179656 | tf_op jit(solution)/shard_map/ppermute | solution.py:222
  345.1 13.3 %collective-permute-start.58 = (bf16[192,384]{1,0:T(8,128)(2,1)S(1)}, bf16[192,384]{1,0:T(8,128)(2,1)S(1)}, u32[]{:S(2)}, u32[]{:S(2)}) collective-permute-start(bf16[192,384]{1,0:T(8,128)(2,1)S(1)} %fusion.72), channel_id=1, source_target_pairs={{0,1},{1,2},{2,3},{3,0},{4,5},{5,6},{6,7},{7,4},{8,9},{9,10},{10,1... | collective-permute-start | bytes 442376 | tf_op jit(solution)/shard_map/ppermute | solution.py:222
  (87 other events, 639.7 us)

commit v2 on v1

v2 whole, which is shorter than its diff:
```python
import functools

import jax
import jax.numpy as jnp
from jax import lax
from jax.experimental import pallas as pl
from jax.experimental.pallas import tpu as pltpu
from jax.sharding import PartitionSpec as P

HEAD_DIM = 64
BLOCK = 256
PAD = 256
RING = 4
EPS = 1e-05
LOG2E = 1.4426950408889634
f32 = jnp.float32
bf16 = jnp.bfloat16
HIDE = -1e30


def nn(a, b):
    return lax.dot_general(a, b, (((1,), (0,)), ((), ())), preferred_element_type=f32)


def nt(a, b):
    return lax.dot_general(a, b, (((1,), (1,)), ((), ())), preferred_element_type=f32)


def doc_of(place, ends):
    return jnp.where(place >= ends[1], 2, jnp.where(place >= ends[0], 1, 0))


def doc_start(row, ends):
    return jnp.where(row >= ends[1], ends[1], jnp.where(row >= ends[0], ends[0], 0))


def hidden_bias(i, j, ends):
    keys = j * BLOCK + lax.broadcasted_iota(jnp.int32, (BLOCK, BLOCK), 0)
    rows = i * BLOCK + lax.broadcasted_iota(jnp.int32, (1, BLOCK), 1)
    start = doc_start(rows, ends)
    stop = jnp.where(rows >= ends[1], 1 << 30, jnp.where(rows >= ends[0], ends[1], ends[0]))
    return jnp.where((keys >= start) & (keys < stop), 0.0, HIDE)


def signed(s, size):
    low = size.astype(bf16)
    return jnp.clip(s.astype(bf16) * bf16(1e38), -low, low)


def ring_blocks(z, count):
    for n in range(count):
        yield n, lax.rem(z - n // 2 + RING, RING) * 2 + n % 2


def walk(i, ends, step, carry):
    def body(j, carry):
        mixed = doc_of(j * BLOCK, ends) != doc_of(i * BLOCK + BLOCK - 1, ends)
        return lax.cond(mixed, lambda c: step(j, c, hidden_bias(i, j, ends)), lambda c: step(j, c, None), carry)

    first = lax.div(doc_start(i * BLOCK, ends), BLOCK)
    return lax.fori_loop(first, i + 1, body, carry)


def head_rows(h, base=0):
    return slice(base + h * HEAD_DIM, base + (h + 1) * HEAD_DIM)


def two_parts(q):
    scaled = q.astype(f32) * (0.125 * LOG2E)
    high = scaled.astype(bf16)
    return high, (scaled - high.astype(f32)).astype(bf16)


def twice(k):
    return jnp.concatenate([k, k], axis=0).T


CHUNK = 64


def chunks():
    return [slice(r, r + CHUNK) for r in range(0, BLOCK, CHUNK)]


def size_of(s, bias, rows):
    a = jnp.abs(s)
    return a if bias is None else a + bias[rows]


def attn_fwd_body(scal, *refs):
    parts, (out, lse, qs, vs, ks, acc, held, low) = refs[:-8], refs[-8:]
    i = pl.program_id(0)
    heads, width = ks.shape[0], vs.shape[1]
    z = scal[0]
    ends = (scal[1], scal[2])

    @pl.when(i == 0)
    def _():
        for n, b in ring_blocks(z, len(parts)):
            ref = parts[n]
            vs[b] = ref[2 * PAD : 2 * PAD + width]
            for h in range(heads):
                high, rest = two_parts(ref[head_rows(h)])
                qs[h, b, 0:HEAD_DIM] = high
                qs[h, b, HEAD_DIM : 2 * HEAD_DIM] = rest
                ks[h, b] = twice(ref[head_rows(h, PAD)])

    acc[...] = jnp.zeros_like(acc)

    def largest(j, carry, bias):
        new = []
        for h in range(heads):
            s = nn(ks[h, j], qs[h, i])
            held[h, j] = s
            top = carry[h]
            for rows in chunks():
                top = jnp.maximum(top, jnp.max(size_of(s[rows], bias, rows).reshape(-1, 8, BLOCK), axis=0))
            new.append(top)
        return tuple(new)

    zero = jnp.zeros((8, BLOCK), f32)
    tops = walk(i, ends, largest, (zero,) * heads)
    tops = [jnp.max(t, axis=0, keepdims=True) for t in tops]

    def weigh(j, carry, bias):
        new = []
        for h in range(heads):
            total = carry[h]
            for rows in chunks():
                s = held[h, j, rows]
                p = jnp.exp2(size_of(s, bias, rows) - tops[h])
                total = total + jnp.sum(p.reshape(-1, 8, BLOCK), axis=0)
                low[h, rows] = signed(s, p)
            new.append(total)
        for h in range(heads):
            acc[head_rows(h)] += nn(vs[j, head_rows(h)], low[h])
        return tuple(new)

    totals = walk(i, ends, weigh, (zero,) * heads)
    t = lax.div(i, 2)
    cols = pl.ds(pl.multiple_of(lax.rem(i, 2) * BLOCK, BLOCK), BLOCK)
    dest = lax.rem(t - z + RING, RING)
    for h in range(heads):
        l = jnp.sum(totals[h], axis=0, keepdims=True)
        out[dest, head_rows(h), cols] = (acc[head_rows(h)] / l).astype(bf16)
        lse[i, h : h + 1, :] = tops[h] + jnp.log(l) * LOG2E


def whole(shape):
    return pl.BlockSpec(shape, lambda *_: (0,) * len(shape))


def sds(shape, dtype=bf16):
    return jax.ShapeDtypeStruct(shape, dtype)


def attn_fwd(scal, parts, heads):
    nb = len(parts)
    width, cols = heads * HEAD_DIM, nb // RING * BLOCK
    return pl.pallas_call(
        attn_fwd_body,
        out_shape=(sds((RING, width, cols)), sds((nb, 8, BLOCK), f32)),
        grid_spec=pltpu.PrefetchScalarGridSpec(
            num_scalar_prefetch=1,
            grid=(nb,),
            in_specs=[whole(p.shape) for p in parts],
            out_specs=(whole((RING, width, cols)), whole((nb, 8, BLOCK))),
            scratch_shapes=[
                pltpu.VMEM((heads, nb, 2 * HEAD_DIM, BLOCK), bf16),
                pltpu.VMEM((nb, width, BLOCK), bf16),
                pltpu.VMEM((heads, nb, BLOCK, 2 * HEAD_DIM), bf16),
                pltpu.VMEM((width, BLOCK), f32),
                pltpu.VMEM((heads, nb, BLOCK, BLOCK), f32),
                pltpu.VMEM((heads, BLOCK, BLOCK), bf16),
            ],
        ),
        compiler_params=pltpu.CompilerParams(dimension_semantics=("arbitrary",)),
        cost_estimate=pl.CostEstimate(flops=5_000_000_000, bytes_accessed=4_000_000, transcendentals=0),
        name="attn_fwd",
    )(scal, *parts)


def attn_bwd_body(scal, *refs):
    parts, refs = refs[:-21], refs[-21:]
    o, g0, g1, g2, g3, lse, grad, q2, qs, kts, gs, ks, vns, inner, dq, dk, dv, held, push, low, dlow = refs
    i = pl.program_id(0)
    nb = pl.num_programs(0)
    heads, width = ks.shape[0], qs.shape[1]
    z = scal[0]
    ends = (scal[1], scal[2])

    @pl.when(i == 0)
    def _():
        for n, b in ring_blocks(z, len(parts)):
            ref = parts[n]
            qs[b] = ref[0:width] * bf16(0.125)
            kts[b] = ref[PAD : PAD + width]
            for h in range(heads):
                high, low = two_parts(ref[head_rows(h)])
                q2[h, b, 0:HEAD_DIM] = high
                q2[h, b, HEAD_DIM : 2 * HEAD_DIM] = low
                ks[h, b] = twice(ref[head_rows(h, PAD)])
                vns[h, b] = ref[head_rows(h, 2 * PAD)].T
        for s, ref in enumerate((g0, g1, g2, g3)):
            t = lax.rem(z + s, RING)
            for half in range(2):
                cols = slice(half * BLOCK, (half + 1) * BLOCK)
                gs[t * 2 + half] = ref[:, cols]
                both = ref[:, cols].astype(f32) * o[s, :, cols].astype(f32)
                for h in range(heads):
                    inner[t * 2 + half, h : h + 1, :] = jnp.sum(both[head_rows(h)], axis=0, keepdims=True)
        dk[...] = jnp.zeros_like(dk)
        dv[...] = jnp.zeros_like(dv)

    dq[i] = jnp.zeros(dq.shape[1:], f32)

    bounds, levers = [], []
    for h in range(heads):
        part = inner[i, h : h + 1, :]
        bounds.append(jnp.abs(part))
        levers.append(jnp.where(part < 0, -1e38, 1e38))

    def products(j, h):
        held[h] = nn(ks[h, j], q2[h, i])
        push[h] = nn(vns[h, j], gs[i, head_rows(h)])

    def step(j, carry, bias):
        products(j, 0)
        for h in range(heads):
            if h + 1 < heads:
                products(j, h + 1)
            for rows in chunks():
                s = held[h, rows]
                mag = jnp.exp2(size_of(s, bias, rows) - lse[i, h : h + 1, :])
                low[h, rows] = signed(s, mag)
                ds = mag * (push[h, rows] - jnp.clip(s * levers[h], -bounds[h], bounds[h]))
                dlow[h, rows] = ds.astype(bf16)
            rows = head_rows(h)
            dv[j, rows] += nt(gs[i, rows], low[h])
            dk[j, rows] += nt(qs[i, rows], dlow[h])
            dq[i, rows] += nn(kts[j, rows], dlow[h])
        return carry

    walk(i, ends, step, 0)

    @pl.when(i == nb - 1)
    def _():
        grad[...] = jnp.zeros_like(grad)
        for n, b in ring_blocks(z, len(parts)):
            cols = slice(n * BLOCK, (n + 1) * BLOCK)
            grad[0:width, cols] = (dq[b] * 0.125).astype(bf16)
            grad[PAD : PAD + width, cols] = dk[b].astype(bf16)
            grad[2 * PAD : 2 * PAD + width, cols] = dv[b].astype(bf16)


def attn_bwd(scal, parts, attended, grads, lse):
    nb = len(parts)
    width = attended.shape[1]
    heads = width // HEAD_DIM
    ops = (*parts, attended, *grads, lse)
    result = (3 * PAD, nb * BLOCK)
    return pl.pallas_call(
        attn_bwd_body,
        out_shape=sds(result),
        grid_spec=pltpu.PrefetchScalarGridSpec(
            num_scalar_prefetch=1,
            grid=(nb,),
            in_specs=[whole(p.shape) for p in ops],
            out_specs=whole(result),
            scratch_shapes=[
                pltpu.VMEM((heads, nb, 2 * HEAD_DIM, BLOCK), bf16),
                pltpu.VMEM((nb, width, BLOCK), bf16),
                pltpu.VMEM((nb, width, BLOCK), bf16),
                pltpu.VMEM((nb, width, BLOCK), bf16),
                pltpu.VMEM((heads, nb, BLOCK, 2 * HEAD_DIM), bf16),
                pltpu.VMEM((heads, nb, BLOCK, HEAD_DIM), bf16),
                pltpu.VMEM((nb, 8, BLOCK), f32),
                pltpu.VMEM((nb, width, BLOCK), f32),
                pltpu.VMEM((nb, width, BLOCK), f32),
                pltpu.VMEM((nb, width, BLOCK), f32),
                pltpu.VMEM((heads, BLOCK, BLOCK), f32),
                pltpu.VMEM((heads, BLOCK, BLOCK), f32),
                pltpu.VMEM((heads, BLOCK, BLOCK), bf16),
                pltpu.VMEM((heads, BLOCK, BLOCK), bf16),
            ],
        ),
        compiler_params=pltpu.CompilerParams(dimension_semantics=("arbitrary",)),
        cost_estimate=pl.CostEstimate(flops=8_000_000_000, bytes_accessed=8_000_000, transcendentals=0),
        name="attn_bwd",
    )(scal, *ops)


LANE = 128


def call(body, outs, *ops, scratch=(), name=None, flops=1_000_000):
    near = pl.BlockSpec(memory_space=pltpu.VMEM)
    return pl.pallas_call(
        body,
        out_shape=tuple(outs),
        in_specs=[near] * len(ops),
        out_specs=(near,) * len(outs),
        scratch_shapes=list(scratch),
        cost_estimate=pl.CostEstimate(flops=flops, bytes_accessed=100_000, transcendentals=0),
        name=name,
    )(*ops)


def aligned(x, n):
    return pl.multiple_of(x, n)


def after(x, *others):
    return lax.optimization_barrier((x, *others))[0]


def mine_of(k):
    return lax.div(lax.axis_index("dp"), 1 << k) & 1


def pack_body(w_qkv, gain_a, gain_m, w_up, w_down, w_out, qkv, keep, give):
    rows, half = w_up.shape[0], w_up.shape[1] // 2
    width = w_out.shape[0]
    mine = mine_of(0)
    qkv[...] = jnp.zeros_like(qkv)
    for c in range(3):
        qkv[:, c * PAD : c * PAD + width] = w_qkv[c]
    eye = lax.broadcasted_iota(jnp.int32, (rows, rows), 0) == lax.broadcasted_iota(jnp.int32, (rows, rows), 1)
    lane = lax.broadcasted_iota(jnp.int32, (rows, LANE), 1)
    cols = [jnp.sum(jnp.where(eye, g[...].astype(f32), 0.0), axis=1, keepdims=True) for g in (gain_a, gain_m)]
    qkv[:, 3 * PAD :] = jnp.where(lane == 0, cols[0], jnp.where(lane == 1, cols[1], 0.0)).astype(bf16)
    tiles = half // LANE
    for k in range(tiles):
        for to, which in ((keep, mine), (give, 1 - mine)):
            at = which * half + k * LANE
            to[k * rows : (k + 1) * rows] = w_up[:, pl.ds(aligned(at, LANE), LANE)]
            to[(tiles + k) * rows : (tiles + k + 1) * rows] = w_down[pl.ds(aligned(at, LANE), LANE), :].T
    base = 2 * tiles * rows
    back = w_out[...].astype(f32).T.astype(bf16)
    keep[base : base + rows] = back[:, 0:LANE]
    keep[base + rows : base + 2 * rows] = jnp.zeros((rows, LANE), bf16)
    keep[base + rows : base + 2 * rows, 0 : width - LANE] = back[:, LANE:width]


def unpack_qkv_body(near, far, w, gains):
    me = lax.axis_index("dp")
    rows = near.shape[1]
    count = near.shape[0]
    tail = []
    for p in range(2 * count):
        src = near if p < count else far
        mask = 2 * (p % count) + (1 if p >= count else 0)
        w[pl.ds(aligned((me ^ mask) * rows, 32), rows)] = src[p % count, :, : 3 * PAD]
    for b in range(2 * count):
        mask = me ^ b
        part = lax.div(mask, 2)
        col = jnp.where(
            (mask & 1) == 0, near[part, :, 3 * PAD :].astype(f32), far[part, :, 3 * PAD :].astype(f32)
        )
        tail.append(col)
    gains[...] = jnp.concatenate(tail, axis=0).T[0:8]


def norm_qkv_body(xa, xb, w, gains, normed, qa, qb):
    for half, (x, q) in enumerate(((xa, qa), (xb, qb))):
        size = x.shape[0]

        for r in range(0, size, 64):
            v = x[r : r + 64].astype(f32)
            c = v - jnp.mean(v, axis=-1, keepdims=True)
            rstd = lax.rsqrt(jnp.mean(c * c, axis=-1, keepdims=True) + EPS)
            normed[half * size + r : half * size + r + 64] = (c * rstd * gains[0:1]).astype(bf16)

        q[...] = nn(normed[half * size : (half + 1) * size], w[...]).astype(bf16).T


def stack_body(p0, p1, p2, p3, a, b):
    u = b.shape[1] // 2
    for s, p in enumerate((p0, p1, p2, p3)):
        a[s, 0:u] = p[0:u]
        b[s, 0:u] = p[u : 2 * u]
        a[s, u : 2 * u] = p[2 * u : 3 * u]
        b[s, u : 2 * u] = p[3 * u : 4 * u]
        a[s, 2 * u :] = p[4 * u :]


def unpack_body(*refs):
    ups, downs, (up, down, back) = refs[0:4], refs[4:8], refs[8:11]
    me = lax.axis_index("dp")
    rows = 96
    half = up.shape[1] // RING
    tiles = half // LANE
    span = tiles * rows
    for p in range(4):
        a, b = ups[p], downs[p]
        for rc in range(2):
            to_a = pl.ds(aligned((me ^ (2 * p + rc)) * rows, 32), rows)
            to_b = pl.ds(aligned((me ^ (2 * ((p & 1) * 2 + (p >> 1)) + rc)) * rows, 32), rows)
            for s in range(RING):
                for k in range(tiles):
                    cols = slice(s * half + k * LANE, s * half + (k + 1) * LANE)
                    src = slice(rc * span + k * rows, rc * span + (k + 1) * rows)
                    up[to_a, cols] = a[s, src]
                    down[to_b, cols] = b[s, src]
        where = lax.div(me ^ (2 * p), 2)
        for s in range(RING):
            for k in range(2):
                back[where, s, :, k * LANE : (k + 1) * LANE] = a[s, 2 * span + k * rows : 2 * span + (k + 1) * rows]


def project_body(x, a0, a1, a2, a3, near, far, gains, mixed, mlp, tokens_major, w):
    mine = mine_of(0)
    rows = near.shape[2]
    width = a0.shape[0]
    for b in range(near.shape[0]):
        for s in range(RING):
            w[s, pl.ds(aligned((2 * b + mine) * rows, 32), rows)] = near[b, s]
            w[s, pl.ds(aligned((2 * b + 1 - mine) * rows, 32), rows)] = far[b, s]
    zero = jnp.zeros((PAD - width, a0.shape[1]), bf16)
    for s, a in enumerate((a0, a1, a2, a3)):
        tokens_major[:, s * PAD : (s + 1) * PAD] = jnp.concatenate([a[...], zero], axis=0).T
    for r in range(0, x.shape[0], 128):
        total = x[r : r + 128].astype(f32)
        for s in range(RING):
            total = total + nt(tokens_major[r : r + 128, s * PAD : (s + 1) * PAD], w[s])
        mixed[r : r + 128] = total
    normalise(mixed, gains[1:2], mlp)


def normalise(rows, gain, out):
    for r in range(0, rows.shape[0], 64):
        at = slice(r, r + 64)
        v = rows[at]
        c = v - jnp.mean(v, axis=-1, keepdims=True)
        rstd = lax.rsqrt(jnp.mean(c * c, axis=-1, keepdims=True) + EPS)
        out[at] = (c * rstd * gain).astype(bf16)


def gelu_both(v):
    square = v * v
    t = jnp.tanh(v * (0.7978845608028654 + (0.7978845608028654 * 0.044715) * square))
    gate = 0.5 + 0.5 * t
    bend = v * (2 * 0.7978845608028654 + (6 * 0.7978845608028654 * 0.044715) * square)
    return v * gate, gate + gate * (1.0 - gate) * bend


def mlp_body(x0, x1, g0, g1, up, down, active, grad, hid, push):
    size = x0.shape[0]
    for half, (x, g) in enumerate(((x1, g1), (x0, g0))):
        hid[half] = nn(x[...], up[...])
        push[half] = nn(g[...], down[...])
    for half in range(2):
        for r in range(0, size, 64):
            rows = slice(r, r + 64)
            to = slice((1 - half) * size + r, (1 - half) * size + r + 64)
            value, slope = gelu_both(hid[half, rows])
            active[to] = value.astype(bf16)
            grad[to] = (push[half, rows] * slope).astype(bf16)


def mlp(x0, x1, g0, g1, up, down):
    tokens, dim = x0.shape
    hidden = up.shape[1]
    keep = pl.BlockSpec((tokens, dim), lambda n: (0, 0))
    cols = pl.BlockSpec((dim, BLOCK), lambda n: (0, n))
    wide = pl.BlockSpec((2 * tokens, BLOCK), lambda n: (0, n))
    return pl.pallas_call(
        mlp_body,
        out_shape=(sds((2 * tokens, hidden)), sds((2 * tokens, hidden))),
        grid=(hidden // BLOCK,),
        in_specs=[keep] * 4 + [cols] * 2,
        out_specs=(wide, wide),
        scratch_shapes=[pltpu.VMEM((2, tokens, BLOCK), f32), pltpu.VMEM((2, tokens, BLOCK), f32)],
        cost_estimate=pl.CostEstimate(flops=5_000_000_000, bytes_accessed=4_000_000, transcendentals=0),
        name="mlp",
    )(x0, x1, g0, g1, up, down)


def rows_by_body(a, w, out, *, start):
    for r in range(0, out.shape[0], 128):
        out[r : r + 128] = nt(a[start + r : start + r + 128], w[...]).astype(out.dtype)


def rows_by(a, w, start, count, dtype, name):
    body = functools.partial(rows_by_body, start=start)
    return call(body, [sds((count, w.shape[0]), dtype)], a, w, name=name)[0]


def norm_back(v, gain, grad):
    c = v - jnp.mean(v, axis=-1, keepdims=True)
    rstd = lax.rsqrt(jnp.mean(c * c, axis=-1, keepdims=True) + EPS)
    hat = c * rstd
    g = grad * gain
    return rstd * (g - jnp.mean(g, axis=-1, keepdims=True) - hat * jnp.mean(g * hat, axis=-1, keepdims=True))


def branch_body(mixed, part, far, grad_out, gains, w, grad_mixed, branch, heads):
    for r in range(0, mixed.shape[0], 64):
        at = slice(r, r + 64)
        grad = part[at] + far[at].astype(f32)
        total = grad_out[at].astype(f32) + norm_back(mixed[at], gains[1:2], grad)
        grad_mixed[at] = total
        branch[at] = total.astype(bf16)

    width = heads.shape[1]
    for s in range(RING):
        heads[s] = nn(branch[...], w[s]).astype(bf16).T[0:width]


def back_body(grad, w, out, *, blocks):
    for k, n in enumerate(blocks):
        out[k] = nt(grad[:, n * BLOCK : (n + 1) * BLOCK].T, w[...]).astype(bf16)


def finish_body(part, recv, x, grad_mixed, gains, out):
    for r in range(0, x.shape[0], 64):
        at = slice(r, r + 64)
        grad = part[at].astype(f32) + recv[at].astype(f32)
        out[at] = grad_mixed[at] + norm_back(x[at].astype(f32), gains[0:1], grad)


def turn(x, shift):
    return lax.ppermute(x, "tensor", [(i, (i + shift) % RING) for i in range(RING)])


def swap(x, axis, bit, size):
    return lax.ppermute(x, axis, [(i, i ^ bit) for i in range(size)])


def pick(x, index, axis=0):
    return lax.dynamic_index_in_dim(x, index, axis, keepdims=False)


def ring_gather(x):
    got = [x]
    for _ in range(RING - 1):
        got.append(turn(got[-1], 1))
    return got


def ring_reduce(chunks):
    moving = chunks[1].astype(bf16)
    for r in range(1, RING):
        moved = turn(moving, 1)
        total = moved.astype(f32) + chunks[(r + 1) % RING]
        moving = total.astype(bf16)
    return total


def spread_blocks(x, bits, size):
    for bit in bits:
        x = jnp.concatenate([x, swap(x, "dp", bit, size)])
    return x


def place_of(mask, bits):
    place = 0
    for k, bit in enumerate(bits):
        place = place + jnp.where(mask & bit != 0, 1 << k, 0)
    return place


def halve(blocks, left, bit, me, size):
    at = left.index(bit)
    lead, tail = 1 << at, 1 << (len(left) - at - 1)
    split = blocks.reshape((lead, 2, tail) + blocks.shape[1:])
    mine = jnp.where(me & bit != 0, 1, 0)
    send = pick(split, 1 - mine, 1).astype(bf16)
    keep = pick(split, mine, 1)
    total = keep.astype(f32) + swap(send, "dp", bit, size).astype(f32)
    return total.reshape((lead * tail,) + blocks.shape[1:]), [b for b in left if b != bit]


def centre(rows):
    shifted = rows - jnp.mean(rows, axis=-1, keepdims=True)
    rstd = lax.rsqrt(jnp.mean(shifted * shifted, axis=-1, keepdims=True) + EPS)
    return shifted * rstd, rstd


def norm_back_plain(grad_hat, hat, rstd):
    return rstd * (
        grad_hat
        - jnp.mean(grad_hat, axis=-1, keepdims=True)
        - hat * jnp.mean(grad_hat * hat, axis=-1, keepdims=True)
    )


def einf(spec, a, b):
    return jnp.einsum(spec, a, b, preferred_element_type=f32)


def shards(size, inputs, doc_ids, gain_attn, w_qkv, w_out, gain_mlp, w_up, w_down, grad_out):
    me = lax.axis_index("dp")
    z = lax.axis_index("tensor")
    odd = me & 1
    others = [1 << k for k in range(1, size.bit_length() - 1)]
    documents = doc_ids[0]
    tokens, dim = inputs.shape
    rows = dim // size
    hid = w_up.shape[1]
    half = hid // 2
    width = w_out.shape[0]
    scal = jnp.stack([z, jnp.sum(documents < 1), jnp.sum(documents < 2)]).astype(jnp.int32)

    pieces = [ring_gather(inputs[k : k + BLOCK]) for k in range(0, tokens, BLOCK)]

    gains = jnp.stack([gain_attn, gain_mlp])
    own = jnp.concatenate([w_qkv[0], w_qkv[1], w_qkv[2], jnp.pad(gains, ((0, 62), (0, 0))).T], axis=1)
    order = others + [1]
    spread_qkv = spread_blocks(own[None], order, size)
    full = jnp.concatenate([pick(spread_qkv, place_of(me ^ b, order)) for b in range(size)])
    full_qkv = full[:, : 3 * width]
    gain_one = full[:, 3 * width].astype(f32)
    gain_two = full[:, 3 * width + 1].astype(f32)

    out_rows = jnp.concatenate([w_out.T[: rows // 2], w_out.T[rows // 2 :]], axis=1)

    def pair_half(w):
        parts = w.reshape(rows, 2, half)
        return jnp.concatenate([pick(parts, odd, 1), swap(pick(parts, 1 - odd, 1), "dp", 1, size)])

    pack_a = jnp.concatenate([pair_half(w_up), out_rows])
    pack_b = pair_half(w_down.T)
    ring_a = jnp.stack(ring_gather(pack_a))
    ring_b = jnp.stack(ring_gather(pack_b))
    order_b = others[::-1]
    spread_a = spread_blocks(ring_a[None], others, size)
    spread_b = spread_blocks(ring_b[None], order_b, size)

    def assemble(spread_w, bits):
        blocks = []
        for b in range(size):
            mask = me ^ b
            block = pick(spread_w, place_of(mask, bits))[:, : 2 * rows]
            block = pick(block.reshape(RING, 2, rows, half), mask & 1, 1)
            blocks.append(block.transpose(1, 0, 2).reshape(rows, RING * half))
        return jnp.concatenate(blocks)

    full_up = assemble(spread_a, others)
    full_down = assemble(spread_b, order_b)
    out_part = spread_a[:, :, 2 * rows :]
    out_both = jnp.stack([out_part, swap(out_part, "dp", 1, size)])

    def out_block(b):
        mask = me ^ b
        block = pick(pick(out_both, mask & 1), place_of(mask, others))
        block = jnp.concatenate([block[..., :width], block[..., width:]], axis=1)
        return block.transpose(1, 0, 2).reshape(rows, RING * width)

    full_out = jnp.concatenate([out_block(b) for b in range(size)])
    grad_both = jnp.concatenate([grad_out, swap(grad_out, "dp", 1, size)])
    grad_active = einf("td,df->tf", grad_both, full_down)

    normed = []
    parts = []
    for s in range(RING):
        for piece in pieces:
            hat, _ = centre(piece[s].astype(f32))
            normed.append((hat * gain_one).astype(bf16))
            part = einf("de,td->et", full_qkv, normed[-1]).astype(bf16).reshape(3, width, BLOCK)
            parts.append(jnp.pad(part, ((0, 0), (0, PAD - width), (0, 0))).reshape(3 * PAD, BLOCK))
    normed = jnp.concatenate(normed)
    sent, lse = attn_fwd(scal, parts, width // HEAD_DIM)
    attended = jnp.concatenate([sent[0]] + [turn(sent[s], s) for s in range(1, RING)])
    mixed = inputs.astype(f32) + einf("et,de->td", attended, full_out)
    hat_two, rstd_two = centre(mixed)
    mlp_rows = (hat_two * gain_two).astype(bf16)
    mlp_both = jnp.concatenate([mlp_rows, swap(mlp_rows, "dp", 1, size)])
    hidden = einf("td,df->tf", mlp_both, full_up)
    value, slope = gelu_both(hidden)
    active = value.astype(bf16)
    grad_hidden = (grad_active * slope).astype(bf16)
    grad_part = einf("tf,df->td", grad_hidden, full_up)
    grad_mlp = grad_part[:tokens] + swap(grad_part[tokens:].astype(bf16), "dp", 1, size).astype(f32)
    grad_mixed = grad_out.astype(f32) + norm_back_plain(grad_mlp * gain_two, hat_two, rstd_two)
    grad_branch = grad_mixed.astype(bf16)
    grad_att = einf("de,td->et", full_out, grad_branch).astype(bf16).reshape(RING, width, tokens)
    grads = [grad_att[0]] + [turn(grad_att[s], -s) for s in range(1, RING)]

    out_pair = einf("tf,df->td", active, full_down)
    layer_out = (
        mixed + out_pair[:tokens] + swap(out_pair[tokens:].astype(bf16), "dp", 1, size).astype(f32)
    ).astype(bf16)

    bits = [1 << k for k in reversed(range(size.bit_length() - 1))]

    def scatter(grad, stages, last_width):
        blocks, left = grad.reshape(size, rows, grad.shape[1]), list(bits)
        for bit in stages:
            blocks, left = halve(blocks, left, bit, me, size)
        blocks = blocks.reshape(-1, blocks.shape[-1])
        return ring_reduce([blocks[:, s * last_width : (s + 1) * last_width] for s in range(RING)])

    def pair_whole(block):
        block = block.reshape(2, rows, half)
        send = pick(block, 1 - odd).astype(bf16)
        keep = pick(block, odd)
        other = swap(send, "dp", 1, size).astype(f32)
        return jnp.where(odd == 0, jnp.concatenate([keep, other], axis=1), jnp.concatenate([other, keep], axis=1))

    grad_down = pair_whole(scatter(einf("td,tf->df", grad_both, active), others, half)).T
    grad_up = pair_whole(scatter(einf("td,tf->df", mlp_both, grad_hidden), order_b, half))
    grad_o = scatter(einf("td,et->de", grad_branch, attended), [1] + order_b, width).T

    grad_parts = attn_bwd(scal, parts, sent, grads, lse)
    grad_parts = grad_parts.reshape(3, PAD, -1)[:, :width].reshape(3 * width, -1)
    grad_proj = einf("td,et->de", normed, grad_parts)
    blocks, left = grad_proj.reshape(size, rows, 3 * width), list(bits)
    for bit in [1] + order_b:
        blocks, left = halve(blocks, left, bit, me, size)
    grad_qkv = blocks[0].reshape(rows, 3, width).transpose(1, 0, 2)

    back = []
    for k in range(0, tokens, BLOCK):
        back.append(
            ring_reduce(
                [
                    einf("et,de->td", grad_parts[:, s * tokens + k : s * tokens + k + BLOCK], full_qkv)
                    for s in range(RING)
                ]
            )
        )
    grad_normed = jnp.concatenate(back)
    hat_one, rstd_one = centre(inputs.astype(f32))
    grad_inputs = grad_mixed + norm_back_plain(grad_normed * gain_one, hat_one, rstd_one)

    sums = jnp.stack(
        [
            jnp.sum(w_qkv.astype(f32) * grad_qkv, axis=(0, 2)),
            jnp.sum(w_up.astype(f32) * grad_up, axis=1),
        ]
    )
    for bit in (1, 2):
        sums = sums + swap(sums, "tensor", bit, RING)
    sums = sums / gains.astype(f32)
    return layer_out, grad_inputs, sums[0], grad_qkv, grad_o, sums[1], grad_up, grad_down


def add(a, b):
    return (a.astype(f32) + b.astype(f32)).astype(bf16)


def first_body(full, recv, send, keep, *, by_y):
    c = mine_of(0)
    mine = mine_of(2 if by_y else 1)
    for k in range(2):
        for which, to in ((mine, keep), (1 - mine, send)):
            at = which * 2 + k if by_y else k * 2 + which
            to[k] = add(full[at * 2 + c], recv[at])


def second_body(keep_in, recv, send, keep):
    mine = mine_of(1)
    keep[...] = add(keep_in[mine], recv[mine])
    send[...] = add(keep_in[1 - mine], recv[1 - mine])


def third_body(up, far_up, down, far_down, o, far_o, up_send, up_keep, mix_send, mix_keep):
    c, x, y = mine_of(0), mine_of(1), mine_of(2)
    rows = up.shape[1]
    tiles = up.shape[2] // RING // LANE
    span = tiles * rows
    for s in range(RING):
        for rc in range(2):
            side = jnp.bitwise_xor(c, rc)
            for k in range(tiles):
                cols = slice((s * tiles + k) * LANE, (s * tiles + k + 1) * LANE)
                to = slice(rc * span + k * rows, rc * span + (k + 1) * rows)
                for which, out in ((x, up_keep), (1 - x, up_send)):
                    out[s, to] = add(up[y * 4 + which * 2 + side, :, cols], far_up[which * 2 + side, :, cols])
                for which, out in ((y, mix_keep), (1 - y, mix_send)):
                    out[s, to] = add(down[which * 4 + x * 2 + side, :, cols], far_down[which * 2 + side, :, cols])
        for k in range(2):
            cols = slice((s * 2 + k) * LANE, (s * 2 + k + 1) * LANE)
            to = slice(2 * span + k * rows, 2 * span + (k + 1) * rows)
            for which, out in ((y, mix_keep), (1 - y, mix_send)):
                out[s, to] = add(o[which, :, cols], far_o[which, :, cols])


def fourth_body(up, far_up, mix, far_mix, first, rest):
    span = up.shape[1] // 2
    extra = mix.shape[1] - 2 * span
    for s in range(RING):
        for rc in range(2):
            src = slice(rc * span, (rc + 1) * span)
            at = rc * 2 * span
            rest[s, at : at + span] = add(up[s, src], far_up[s, src])
            rest[s, at + span : at + 2 * span] = add(mix[s, src], far_mix[s, src])
        tail = slice(2 * span, 2 * span + extra)
        rest[s, 4 * span : 4 * span + extra] = add(mix[s, tail], far_mix[s, tail])
    first[...] = rest[1]


def fifth_body(mine, far, up, down, o):
    c = mine_of(0)
    rows = up.shape[0]
    half = up.shape[1] // 2
    tiles = half // LANE
    for side, src in ((c, mine), (1 - c, far)):
        for k in range(tiles):
            at = pl.ds(aligned(side * half + k * LANE, LANE), LANE)
            up[:, at] = src[k * rows : (k + 1) * rows].astype(f32)
            down[at, :] = src[(tiles + k) * rows : (tiles + k + 1) * rows].astype(f32).T
    base = 4 * tiles * rows
    width = o.shape[0]
    o[0:LANE] = mine[base : base + rows].astype(f32).T
    o[LANE:width] = mine[base + rows : base + 2 * rows].astype(f32).T[0 : width - LANE]


def shards_small(size, inputs, doc_ids, gain_attn, w_qkv, w_out, gain_mlp, w_up, w_down, grad_out):
    me = lax.axis_index("dp")
    z = lax.axis_index("tensor")
    documents = doc_ids[0]
    tokens, dim = inputs.shape
    rows, hid = w_up.shape
    half = hid // 2
    width = w_out.shape[0]
    heads = width // HEAD_DIM
    hidden = RING * half
    scal = jnp.stack([z, jnp.sum(documents < 1), jnp.sum(documents < 2)]).astype(jnp.int32)

    def pair(x):
        return swap(x, "dp", 1, size)

    def along_x(x):
        return swap(x, "dp", 2, size)

    def along_y(x):
        return swap(x, "dp", 4, size)

    span = half * rows // LANE
    x_a, x_b = ([inputs[k : k + BLOCK]] for k in range(0, tokens, BLOCK))
    x_a.append(turn(x_a[0], 1))
    x_b.append(turn(x_b[0], 1))
    qkv, keep, give = call(
        pack_body,
        [sds((rows, 3 * PAD + LANE)), sds((2 * span + 2 * rows, LANE)), sds((2 * span, LANE))],
        w_qkv, gain_attn[None], gain_mlp[None], w_up, w_down, w_out, name="pack",
    )
    got = pair(give)
    qkv = jnp.stack([qkv, along_x(qkv)])
    packed = jnp.concatenate([keep[: 2 * span], got, keep[2 * span :]])
    ring = [packed, turn(packed, 1)]
    qkv = jnp.concatenate([qkv, along_y(qkv)])
    qkv_far = pair(qkv)
    x_a.append(turn(x_a[1], 1))
    x_b.append(turn(x_b[1], 1))
    ring.append(turn(after(ring[1], x_a[1], x_b[1]), 1))
    full_qkv, gains = call(
        unpack_qkv_body, [sds((dim, 3 * PAD)), sds((8, dim), f32)], qkv, qkv_far, name="unpack_qkv"
    )
    normed, parts = [], []

    def attention_rows(s):
        n, qa, qb = call(
            norm_qkv_body,
            [sds((tokens, dim)), sds((3 * PAD, BLOCK)), sds((3 * PAD, BLOCK))],
            x_a[s], x_b[s], full_qkv, gains, name="norm_qkv",
        )
        normed.append(n)
        parts.extend((qa, qb))
        return n

    attention_rows(0)
    ring.append(turn(after(ring[2], normed[0], x_a[2]), 1))
    grad_far = pair(grad_out)
    attention_rows(1)
    x_a.append(turn(x_a[2], 1))
    x_b.append(turn(x_b[2], 1))
    ups0, downs0 = call(
        stack_body,
        [sds((RING, 2 * span + 2 * rows, LANE)), sds((RING, 2 * span, LANE))],
        *ring[:3], after(ring[3], normed[1], x_b[2]), name="stack",
    )
    ups1, downs1 = along_x(ups0), along_y(downs0)
    ups2, downs2 = along_y(ups0), along_x(downs0)
    attention_rows(2)
    ups3, downs3 = along_y(after(ups1, normed[2])), along_x(after(downs1, normed[2]))
    attention_rows(3)

    sent, lse = attn_fwd(scal, parts, heads)
    attended = [sent[0]] + [turn(sent[s], s) for s in range(1, RING)]
    full_up, full_down, back_near = call(
        unpack_body,
        [sds((dim, hidden)), sds((dim, hidden)), sds((size // 2, RING, rows, PAD))],
        ups0, ups1, ups2, after(ups3, sent), downs0, downs1, downs2, after(downs3, sent), name="unpack",
    )
    back_far = pair(back_near)
    mixed, mlp_rows, att_tokens, full_out = call(
        project_body,
        [sds((tokens, dim), f32), sds((tokens, dim)), sds((tokens, RING * PAD)), sds((RING, dim, PAD))],
        inputs, *attended, back_near, back_far, gains, name="project",
    )
    mlp_far = pair(mlp_rows)
    active, grad_hidden = mlp(mlp_rows, mlp_far, grad_out, grad_far, full_up, full_down)
    part_far = rows_by(grad_hidden, full_up, tokens, tokens, bf16, "part_far")
    part_got = pair(part_far)
    part = rows_by(after(grad_hidden, part_far), full_up, 0, tokens, f32, "part")
    grad_mixed, branch, grad_att = call(
        branch_body,
        [sds((tokens, dim), f32), sds((tokens, dim)), sds((RING, width, tokens))],
        mixed, part, part_got, grad_out, gains, full_out, name="branch",
    )
    grads = [grad_att[0]] + [turn(grad_att[s], -s) for s in range(1, RING)]
    grad_hidden_late = after(grad_hidden, grads[1])
    active_late = after(active, grads[1])
    tokens_late = after(att_tokens, grads[2])

    x_bit, y_bit, c_bit = lax.div(me, 2) & 1, lax.div(me, 4) & 1, me & 1
    both_in = jnp.concatenate([mlp_rows, mlp_far])
    both_grad = jnp.concatenate([grad_out, grad_far])
    grad_up = einf("td,tf->df", both_in, grad_hidden_late).astype(bf16)
    grad_down = einf("td,tf->df", both_grad, active_late).astype(bf16)
    grad_o = einf("td,te->de", branch, tokens_late).astype(bf16)
    far_up = along_y(pick(grad_up.reshape(2, 4, rows, hidden), 1 - y_bit))
    far_down = along_x(pick(grad_down.reshape(2, 2, 2, rows, hidden), 1 - x_bit, 1).reshape(4, rows, hidden))
    far_o = pair(pick(grad_o.reshape(4, 2, rows, RING * PAD), 1 - c_bit, 1))
    o_shape = [sds((2, rows, RING * PAD))] * 2
    o_send, o_keep = call(
        functools.partial(first_body, by_y=False),
        o_shape, grad_o.reshape(size, rows, RING * PAD), far_o, name="first_o",
    )
    layer_far = pair(rows_by(after(active, grads[3]), full_down, tokens, tokens, bf16, "out_far"))
    layer_near = rows_by(after(active, grads[3]), full_down, 0, tokens, f32, "out_near")
    layer_out = (mixed + layer_near + layer_far.astype(f32)).astype(bf16)

    grad_parts = attn_bwd(scal, parts, sent, grads, after(lse, layer_near, o_keep, far_o))
    count = tokens // BLOCK

    def backs(blocks, name):
        return call(
            functools.partial(back_body, blocks=blocks),
            [sds((len(blocks), BLOCK, dim))], grad_parts, full_qkv, name=name,
        )[0]

    start = backs(list(range(count, 2 * count)), "back_first")
    later = backs(list(range(2 * count, RING * count)) + list(range(count)), "back_rest")
    came = [turn(start[k], 1) for k in range(count)]
    up_shape, mix_shape = sds((RING, 2 * span, LANE)), sds((RING, 2 * span + 2 * rows, LANE))
    up_send, up_keep, mix_send, mix_keep = call(
        third_body,
        [up_shape, up_shape, mix_shape, mix_shape],
        grad_up.reshape(size, rows, hidden), after(far_up, came[0]), grad_down.reshape(size, rows, hidden), far_down,
        o_keep, along_x(o_send), name="third",
    )
    came = [turn(add(later[k], came[k]), 1) for k in range(count)]
    total_shape = (4 * span + 2 * rows, LANE)
    moving, rest = call(
        fourth_body,
        [sds(total_shape), sds((RING, *total_shape))],
        up_keep, after(along_x(up_send), came[1]), mix_keep, along_y(mix_send), name="fourth",
    )

    came = [turn(add(later[count + k], came[k]), 1) for k in range(count)]
    grad_inputs = jnp.concatenate(
        [
            call(
                finish_body,
                [sds((BLOCK, dim), f32)],
                later[(RING - 2) * count + k], came[k], inputs[k * BLOCK : (k + 1) * BLOCK],
                grad_mixed[k * BLOCK : (k + 1) * BLOCK], gains, name="finish",
            )[0]
            for k in range(count)
        ]
    )

    grad_proj = einf("td,et->de", jnp.concatenate(normed), grad_parts).astype(bf16)
    far_qkv = pair(pick(grad_proj.reshape(4, 2, rows, 3 * PAD), 1 - c_bit, 1))
    q_send, q_keep = call(
        functools.partial(first_body, by_y=True),
        [sds((2, rows, 3 * PAD))] * 2, grad_proj.reshape(size, rows, 3 * PAD), far_qkv, name="first_qkv",
    )
    q_send, q_keep = call(
        second_body, [sds((rows, 3 * PAD))] * 2, q_keep, along_y(q_send), name="second_qkv"
    )
    grad_flat = q_keep.astype(f32) + along_x(q_send).astype(f32)
    grad_qkv = jnp.stack([grad_flat[:, c * PAD : c * PAD + width] for c in range(3)])

    for r in range(1, RING):
        moving = add(turn(moving, 1), rest[(r + 1) % RING])
    grad_up, grad_down, grad_o = call(
        fifth_body,
        [sds((rows, hid), f32), sds((hid, rows), f32), sds((width, rows), f32)],
        moving, pair(moving[2 * span : 4 * span]), name="fifth",
    )
    sums = jnp.stack(
        [
            jnp.sum(w_qkv.astype(f32) * grad_qkv, axis=(0, 2)),
            jnp.sum(w_up.astype(f32) * grad_up, axis=1),
        ]
    )
    for bit in (1, 2):
        sums = sums + swap(sums, "tensor", bit, RING)
    own = jnp.stack([gain_attn, gain_mlp]).astype(f32)
    sums = sums / own
    return layer_out, grad_inputs, sums[0], grad_qkv, grad_o, sums[1], grad_up, grad_down
def solution(mesh):
    both = P(("dp", "tensor"), None)
    weights = (P(None, "dp", "tensor"), P("tensor", "dp"), P("dp"), P("dp", "tensor"), P("tensor", "dp"))
    return jax.shard_map(
        functools.partial(shards_small if mesh.shape["dp"] == 8 else shards, mesh.shape["dp"]),
        mesh=mesh,
        in_specs=(both, P("dp", None), P("dp"), *weights, both),
        out_specs=(both, both, P("dp"), *weights),
        check_vma=False,
    )
```

time: 383 us -> 426 us (1.11)
  Pallas kernels: 45.6 us -> 150 us
  waiting for transfers between devices: 98 us -> 158 us
  matrix products: 65.4 us -> 16 us
  other arithmetic: 47 us -> 16.7 us
  local copies, waits for them, and re-layouts: 56.6 us -> 26.4 us
  starting transfers between devices: 60.2 us -> 48.7 us
    pallas_call x2 -> x27, Pallas kernels: 45.7 us -> 150 us  [the longest x24 99.6 us: call(): pl.pallas_call(body, out_shape=tuple(outs), in_specs=[near] * len(ops), o...]
    dot_general x26 -> x4, matrix products: 65.4 us -> 16 us  [einf(): return jnp.einsum(spec, a, b, preferred_element_type=f32)]
    ppermute x28 -> x27, waiting for transfers between devices: 17.4 us -> 65.5 us  [swap(): return lax.ppermute(x, axis, [(i, i ^ bit) for i in range(size)])]
    add x14 -> x2, other arithmetic: 16.2 us -> 0.04 us  [the longest x1 0.03 us: shards_small(): grad_flat = q_keep.astype(f32) + along_x(q_send).astype(f32)]
    ppermute x33 -> x24, waiting for transfers between devices: 80.5 us -> 92.6 us  [turn(): lax.ppermute(x, 'tensor', [(i, (i + shift) % RING) for i in range(RING)])]
    ppermute x28 -> x27, starting transfers between devices: 28.9 us -> 19.8 us  [swap(): return lax.ppermute(x, axis, [(i, i ^ bit) for i in range(size)])]
    reshape x26 -> x0, local copies, waits for them, and re-layouts: 8.87 us -> none  [the longest x8 6.47 us: out_block(): return block.transpose(1, 0, 2).reshape(rows, RING * width)]
    convert_element_type x11 -> x0, local copies, waits for them, and re-layouts: 8.87 us -> none  [the longest x9 8.83 us: halve(): send = pick(split, 1 - mine, 1).astype(bf16)]
  transfers between devices with their start and end apart: 61 -> 51, of which waited for: 27 -> 26; matrix products, arithmetic and copies ran while one was open for 34% -> 11% of each run, Pallas kernels for 12% -> 28%
where the time goes in v2:
time: 426 us; the launch traced here: 418 us
  waiting for transfers between devices  158 us (37%)
  Pallas kernels  150 us (35%)
  starting transfers between devices  48.7 us (11%)
  local copies, waits for them, and re-layouts  26.4 us (6%)
  other arithmetic  16.7 us (4%)
  matrix products  16 us (4%)
    pallas_call x24, Pallas kernels, call(): pl.pallas_call(body, out_shape=tuple(outs), in_specs=[near] * len(ops), o...  99.6 us
    ppermute x24, waiting for transfers between devices, turn(): lax.ppermute(x, 'tensor', [(i, (i + shift) % RING) for i in range(RING)])  92.6 us
    ppermute x27, waiting for transfers between devices, swap(): return lax.ppermute(x, axis, [(i, i ^ bit) for i in range(size)])  65.5 us
    ppermute x24, starting transfers between devices, turn(): lax.ppermute(x, 'tensor', [(i, (i + shift) % RING) for i in range(RING)])  28.9 us
    pallas_call x1, Pallas kernels, attn_bwd(): pl.pallas_call(attn_bwd_body, out_shape=sds(result), grid_spec=pltpu.Pref...  23 us
    ppermute x27, starting transfers between devices, swap(): return lax.ppermute(x, axis, [(i, i ^ bit) for i in range(size)])  19.8 us
    pallas_call x1, Pallas kernels, attn_fwd(): pl.pallas_call(attn_fwd_body, out_shape=(sds((RING, width, cols)), sds((n...  16.6 us
    dot_general x4, matrix products, einf(): return jnp.einsum(spec, a, b, preferred_element_type=f32)  16 us
  transfers between devices with their start and end apart: 51, of which 26 were waited for; matrix products, arithmetic and copies ran while one was open for 11% of the time, Pallas kernels for 28%

profile of v2, /device:TPU:0, one launch (start us, length us, event | category | flops | bytes accessed | tf_op | source)
XLA Modules:
  0.0 417.9 jit_solution(14671878260144330651)
XLA Ops:
  24.0 5.7 %collective-permute-done.3.xa = bf16[256,768]{1,0:T(8,128)(2,1)S(1)} collective-permute-done((bf16[256,768]{1,0:T(8,128)(2,1)S(1)}, bf16[256,768]{1,0:T(8,128)(2,1)S(1)}, u32[]{:S(2)}, u32[]{:S(2)}) %collective-permute-start.3) | collective-permute-done | bytes 393248 | tf_op jit(solution)/shard_map/ppermute | solution.py:523
  29.8 8.5 %collective-permute-done.4.xb = bf16[256,768]{1,0:T(8,128)(2,1)} collective-permute-done((bf16[256,768]{1,0:T(8,128)(2,1)S(1)}, bf16[256,768]{1,0:T(8,128)(2,1)}, u32[]{:S(2)}, u32[]{:S(2)}) %collective-permute-start.4) | collective-permute-done | bytes 393248 | tf_op jit(solution)/shard_map/ppermute | solution.py:523
  38.3 7.4 %collective-permute-done.13.p1 = bf16[1344,128]{1,0:T(8,128)(2,1)} collective-permute-done((bf16[1344,128]{1,0:T(8,128)(2,1)S(1)}, bf16[1344,128]{1,0:T(8,128)(2,1)}, u32[]{:S(2)}, u32[]{:S(2)}) %collective-permute-start.13) | collective-permute-done | bytes 344096 | tf_op jit(solution)/shard_map/ppermute | solution.py:523
  54.1 7.4 %collective-permute-done.14.p2 = bf16[1344,128]{1,0:T(8,128)(2,1)} collective-permute-done((bf16[1344,128]{1,0:T(8,128)(2,1)}, bf16[1344,128]{1,0:T(8,128)(2,1)}, u32[]{:S(2)}, u32[]{:S(2)}) %collective-permute-start.14) | collective-permute-done | bytes 344096 | tf_op jit(solution)/shard_map/ppermute | solution.py:523
  64.9 4.8 %collective-permute-done.6.xb = bf16[256,768]{1,0:T(8,128)(2,1)S(1)} collective-permute-done((bf16[256,768]{1,0:T(8,128)(2,1)}, bf16[256,768]{1,0:T(8,128)(2,1)S(1)}, u32[]{:S(2)}, u32[]{:S(2)}) %collective-permute-start.6) | collective-permute-done | bytes 393248 | tf_op jit(solution)/shard_map/ppermute | solution.py:523
  69.8 7.0 %collective-permute-done.15.p3 = bf16[1344,128]{1,0:T(8,128)(2,1)S(1)} collective-permute-done((bf16[1344,128]{1,0:T(8,128)(2,1)}, bf16[1344,128]{1,0:T(8,128)(2,1)S(1)}, u32[]{:S(2)}, u32[]{:S(2)}) %collective-permute-start.15) | collective-permute-done | bytes 344096 | tf_op jit(solution)/shard_map/ppermute | solution.py:523
  86.7 12.6 %collective-permute-done.16.refs_1_ = bf16[4,768,128]{2,1,0:T(8,128)(2,1)S(1)} collective-permute-done((bf16[4,768,128]{2,1,0:T(8,128)(2,1)}, bf16[4,768,128]{2,1,0:T(8,128)(2,1)S(1)}, u32[]{:S(2)}, u32[]{:S(2)}) %collective-permute-start.16) | collective-permute-done | bytes 786464 | tf_op jit(solution)/shard_map/ppermute | solution.py:527
  109.5 16.6 %attn_fwd.1 = (bf16[4,192,512]{2,1,0:T(8,128)(2,1)}, f32[8,8,256]{2,1,0:T(8,128)}) custom-call(s32[3]{0:T(128)} %pad_add_fusion.scal, bf16[768,256]{1,0:T(8,128)(2,1)} %get-tuple-element.74.refs_0_, bf16[768,256]{1,0:T(8,128)(2,1)} %get-tuple-element.75.refs_1_, bf16[768,256]{1,0:T(8,128)(2,1)} %get-tuple-element.76.refs_2_, ...), custom_call_target="tpu_custom_call" | custom-call | flops 5000000000 | bytes 4000000 | tf_op jit(solution)/shard_map/attn_fwd/pallas_call | solution.py:160
  128.7 6.0 %collective-permute-done.17.refs_2_ = bf16[4,768,128]{2,1,0:T(8,128)(2,1)} collective-permute-done((bf16[4,768,128]{2,1,0:T(8,128)(2,1)}, bf16[4,768,128]{2,1,0:T(8,128)(2,1)}, u32[]{:S(2)}, u32[]{:S(2)}) %collective-permute-start.17) | collective-permute-done | bytes 786464 | tf_op jit(solution)/shard_map/ppermute | solution.py:527
  134.7 6.0 %unpack.1 = (bf16[768,1536]{1,0:T(8,128)(2,1)}, bf16[768,1536]{1,0:T(8,128)(2,1)}, bf16[4,4,96,256]{3,2,1,0:T(8,128)(2,1)}) custom-call(bf16[4,768,128]{2,1,0:T(8,128)(2,1)} %get-tuple-element.90.refs_0_, bf16[4,768,128]{2,1,0:T(8,128)(2,1)} %copy-done.18, bf16[4,768,128]{2,1,0:T(8,128)(2,1)} %collective-permute-done.17.refs_2_, ...), custom_call_target="tpu_custom_call" | custom-call | flops 1000000 | bytes 100000 | tf_op jit(solution)/shard_map/unpack/pallas_call | solution.py:298
  145.4 5.7 %collective-permute-done.9.a1 = bf16[192,512]{1,0:T(8,128)(2,1)S(1)} collective-permute-done((bf16[192,512]{1,0:T(8,128)(2,1)S(1)}, bf16[192,512]{1,0:T(8,128)(2,1)S(1)}, u32[]{:S(2)}, u32[]{:S(2)}) %collective-permute-start.9) | collective-permute-done | bytes 196640 | tf_op jit(solution)/shard_map/ppermute | solution.py:523
  151.2 7.4 %collective-permute-done.10.a2 = bf16[192,512]{1,0:T(8,128)(2,1)S(1)} collective-permute-done((bf16[192,512]{1,0:T(8,128)(2,1)S(1)}, bf16[192,512]{1,0:T(8,128)(2,1)S(1)}, u32[]{:S(2)}, u32[]{:S(2)}) %collective-permute-start.10) | collective-permute-done | bytes 196640 | tf_op jit(solution)/shard_map/ppermute | solution.py:523
  159.6 6.5 %project.1 = (f32[512,768]{1,0:T(8,128)}, bf16[512,768]{1,0:T(8,128)(2,1)}, bf16[512,1024]{1,0:T(8,128)(2,1)}, bf16[4,768,256]{2,1,0:T(8,128)(2,1)}) custom-call(bf16[512,768]{1,0:T(8,128)(2,1)} %x.1, bf16[192,512]{1,0:T(8,128)(2,1)} %get-tuple-element.161.a0, bf16[192,512]{1,0:T(8,128)(2,1)} %copy-done.35, bf16[192,512]{1,0:T(8,128)(2,1)} %copy-done.36, ...), custom_call_target="tpu_custom_call" | custom-call | flops 1000000 | bytes 100000 | tf_op jit(solution)/shard_map/project/pallas_call | solution.py:298
  169.5 11.2 %mlp.1 = (bf16[1024,1536]{1,0:T(8,128)(2,1)}, bf16[1024,1536]{1,0:T(8,128)(2,1)}) custom-call(bf16[512,768]{1,0:T(8,128)(2,1)} %get-tuple-element.99.x0, bf16[512,768]{1,0:T(8,128)(2,1)} %copy-done.47, bf16[512,768]{1,0:T(8,128)(2,1)} %grad_out.1, bf16[512,768]{1,0:T(8,128)(2,1)} %copy-done.45, bf16[768,1536]{1,0:T(8,128)(2,1)} %get-tuple-element.100.up.w, ...), custom_call_target="tpu_custom_call" | custom-call | flops 5000000000 | bytes 4000000 | tf_op jit(solution)/shard_map/mlp/pallas_call | solution.py:467
  180.7 6.7 %part_far.1 = bf16[512,768]{1,0:T(8,128)(2,1)} custom-call(bf16[1024,1536]{1,0:T(8,128)(2,1)} %get-tuple-element.120.a, bf16[768,1536]{1,0:T(8,128)(2,1)} %get-tuple-element.100.up.w), custom_call_target="tpu_custom_call" | custom-call | flops 1000000 | bytes 100000 | tf_op jit(solution)/shard_map/part_far/pallas_call | solution.py:298
  187.6 7.0 %part.1 = f32[512,768]{1,0:T(8,128)} custom-call(bf16[1024,1536]{1,0:T(8,128)(2,1)} %get-tuple-element.120.a, bf16[768,1536]{1,0:T(8,128)(2,1)} %get-tuple-element.100.up.w), custom_call_target="tpu_custom_call" | custom-call | flops 1000000 | bytes 100000 | tf_op jit(solution)/shard_map/part/pallas_call | solution.py:298
  195.5 5.8 %branch.1 = (f32[512,768]{1,0:T(8,128)}, bf16[512,768]{1,0:T(8,128)(2,1)}, bf16[4,192,512]{2,1,0:T(8,128)(2,1)}) custom-call(f32[512,768]{1,0:T(8,128)} %get-tuple-element.98.mixed, f32[512,768]{1,0:T(8,128)} %part.1, bf16[512,768]{1,0:T(8,128)(2,1)} %copy-done.15, bf16[512,768]{1,0:T(8,128)(2,1)} %grad_out.1, f32[8,768]{1,0:T(8,128)} %get-tuple-element.73.gains, ...), custom_call_target="tpu_custom_call" | custom-call | flops 1000000 | bytes 100000 | tf_op jit(solution)/shard_map/branch/pallas_call | solution.py:298
  210.5 10.2 %collective-permute-done.29.refs_11_ = bf16[192,512]{1,0:T(8,128)(2,1)S(1)} collective-permute-done((bf16[192,512]{1,0:T(8,128)(2,1)S(1)}, bf16[192,512]{1,0:T(8,128)(2,1)S(1)}, u32[]{:S(2)}, u32[]{:S(2)}) %collective-permute-start.29) | collective-permute-done | bytes 196640 | tf_op jit(solution)/shard_map/ppermute | solution.py:523
  230.9 6.9 %out_near.1 = f32[512,768]{1,0:T(8,128)} custom-call(bf16[1024,1536]{1,0:T(8,128)(2,1)} %get-tuple-element.122.a, bf16[768,1536]{1,0:T(8,128)(2,1)} %get-tuple-element.101.down.w), custom_call_target="tpu_custom_call" | custom-call | flops 1000000 | bytes 100000 | tf_op jit(solution)/shard_map/out_near/pallas_call | solution.py:298
  237.8 5.3 %convolution_convert_fusion = bf16[768,1536]{1,0:T(8,128)(2,1)} fusion(bf16[1024,1536]{1,0:T(8,128)(2,1)S(1)} %copy-done, bf16[512,768]{1,0:T(8,128)(2,1)} %copy-done.45, bf16[512,768]{1,0:T(8,128)(2,1)} %grad_out.1), kind=kOutput, calls=%fused_computation | convolution fusion | flops 2420244480 | bytes 7077888 | tf_op jit(solution)/shard_map/td,tf->df/dot_general | solution.py:589
  245.9 23.0 %attn_bwd.1.grad = bf16[768,2048]{1,0:T(8,128)(2,1)} custom-call(s32[3]{0:T(128)} %pad_add_fusion.scal, bf16[768,256]{1,0:T(8,128)(2,1)} %get-tuple-element.74.refs_0_, bf16[768,256]{1,0:T(8,128)(2,1)} %get-tuple-element.75.refs_1_, bf16[768,256]{1,0:T(8,128)(2,1)} %get-tuple-element.76.refs_2_, bf16[768,256]{1,0:T(8,128)(2,1)} %get-tuple-element.77.refs_3_, ...), custom_call_target="tpu_custom_call" | custom-call | flops 8000000000 | bytes 8000000 | tf_op jit(solution)/shard_map/attn_bwd/pallas_call | solution.py:262
  282.5 5.9 %back_rest.1 = bf16[6,256,768]{2,1,0:T(8,128)(2,1)} custom-call(bf16[768,2048]{1,0:T(8,128)(2,1)} %attn_bwd.1.grad, bf16[768,768]{1,0:T(8,128)(2,1)} %get-tuple-element.72.w), custom_call_target="tpu_custom_call" | custom-call | flops 1000000 | bytes 100000 | tf_op jit(solution)/shard_map/back_rest/pallas_call | solution.py:298
  291.1 5.5 %fusion.14 = bf16[768,768]{1,0:T(8,128)(2,1)} fusion(bf16[768,2048]{1,0:T(8,128)(2,1)S(1)} %copy-done.2, bf16[512,768]{1,0:T(8,128)(2,1)} %get-tuple-element.115, bf16[512,768]{1,0:T(8,128)(2,1)} %get-tuple-element.91, bf16[512,768]{1,0:T(8,128)(2,1)} %get-tuple-element.88, bf16[512,768]{1,0:T(8,128)(2,1)} %get-tuple-element.86), kind=kOutput, calls=%fused_computation.19 | convolution fusion | flops 2429091840 | bytes 7471104 | tf_op jit(solution)/shard_map/td,et->de/dot_general | solution.py:589
  296.6 10.5 %collective-permute-done.41.far_down = bf16[4,96,1536]{2,1,0:T(8,128)(2,1)} collective-permute-done((bf16[4,96,1536]{2,1,0:T(8,128)(2,1)}, bf16[4,96,1536]{2,1,0:T(8,128)(2,1)}, u32[]{:S(2)}, u32[]{:S(2)}) %collective-permute-start.41) | collective-permute-done | bytes 1179680 | tf_op jit(solution)/shard_map/ppermute | solution.py:527
  307.1 6.8 %collective-permute-done.42.far_o = bf16[2,96,1024]{2,1,0:T(8,128)(2,1)} collective-permute-done((bf16[2,96,1024]{2,1,0:T(8,128)(2,1)}, bf16[2,96,1024]{2,1,0:T(8,128)(2,1)}, u32[]{:S(2)}, u32[]{:S(2)}) %collective-permute-start.42) | collective-permute-done | bytes 393248 | tf_op jit(solution)/shard_map/ppermute | solution.py:527
  314.0 5.5 %third.1 = (bf16[4,576,128]{2,1,0:T(8,128)(2,1)}, bf16[4,576,128]{2,1,0:T(8,128)(2,1)}, bf16[4,768,128]{2,1,0:T(8,128)(2,1)}, bf16[4,768,128]{2,1,0:T(8,128)(2,1)}) custom-call(bf16[8,96,1536]{2,1,0:T(8,128)(2,1)} %bitcast.99, bf16[4,96,1536]{2,1,0:T(8,128)(2,1)} %collective-permute-done.40.far_up, bf16[8,96,1536]{2,1,0:T(8,128)(2,1)} %bitcast.100, ...), custom_call_target="tpu_custom_call" | custom-call | flops 1000000 | bytes 100000 | tf_op jit(solution)/shard_map/third/pallas_call | solution.py:298
  327.2 10.7 %collective-permute-done.43.far_up = bf16[4,576,128]{2,1,0:T(8,128)(2,1)S(1)} collective-permute-done((bf16[4,576,128]{2,1,0:T(8,128)(2,1)}, bf16[4,576,128]{2,1,0:T(8,128)(2,1)S(1)}, u32[]{:S(2)}, u32[]{:S(2)}) %collective-permute-start.43) | collective-permute-done | bytes 589856 | tf_op jit(solution)/shard_map/ppermute | solution.py:527
  344.5 6.7 %out_far.1 = bf16[512,768]{1,0:T(8,128)(2,1)} custom-call(bf16[1024,1536]{1,0:T(8,128)(2,1)} %get-tuple-element.122.a, bf16[768,1536]{1,0:T(8,128)(2,1)} %get-tuple-element.101.down.w), custom_call_target="tpu_custom_call" | custom-call | flops 1000000 | bytes 100000 | tf_op jit(solution)/shard_map/out_far/pallas_call | solution.py:298
  357.2 6.0 %collective-permute-done.38.recv = bf16[2,96,768]{2,1,0:T(8,128)(2,1)} collective-permute-done((bf16[2,96,768]{2,1,0:T(8,128)(2,1)}, bf16[2,96,768]{2,1,0:T(8,128)(2,1)}, u32[]{:S(2)}, u32[]{:S(2)}) %collective-permute-start.38) | collective-permute-done | bytes 294944 | tf_op jit(solution)/shard_map/ppermute | solution.py:527
  371.3 9.2 %collective-permute-done.46 = bf16[1344,128]{1,0:T(8,128)(2,1)S(1)} collective-permute-done((bf16[1344,128]{1,0:T(8,128)(2,1)S(1)}, bf16[1344,128]{1,0:T(8,128)(2,1)S(1)}, u32[]{:S(2)}, u32[]{:S(2)}) %collective-permute-start.46) | collective-permute-done | bytes 344096 | tf_op jit(solution)/shard_map/ppermute | solution.py:523
  381.6 13.1 %collective-permute-done.47 = bf16[1344,128]{1,0:T(8,128)(2,1)S(1)} collective-permute-done((bf16[1344,128]{1,0:T(8,128)(2,1)S(1)}, bf16[1344,128]{1,0:T(8,128)(2,1)S(1)}, u32[]{:S(2)}, u32[]{:S(2)}) %collective-permute-start.47) | collective-permute-done | bytes 344096 | tf_op jit(solution)/shard_map/ppermute | solution.py:523
  404.0 5.4 %collective-permute-done.36.recv = bf16[256,768]{1,0:T(8,128)(2,1)} collective-permute-done((bf16[256,768]{1,0:T(8,128)(2,1)}, bf16[256,768]{1,0:T(8,128)(2,1)}, u32[]{:S(2)}, u32[]{:S(2)}) %collective-permute-start.36) | collective-permute-done | bytes 393248 | tf_op jit(solution)/shard_map/ppermute | solution.py:523
  (241 shorter events, 153.2 us)
Async XLA Ops:
  17.6 20.7 %collective-permute-start.4 = (bf16[256,768]{1,0:T(8,128)(2,1)S(1)}, bf16[256,768]{1,0:T(8,128)(2,1)}, u32[]{:S(2)}, u32[]{:S(2)}) collective-permute-start(bf16[256,768]{1,0:T(8,128)(2,1)S(1)} %get-tuple-element.162.xb.x), channel_id=1, source_target_pairs={{0,1},{1,2},{2,3},{3,0},{4,5},{5,6},{6,7},{7,4},{8,9},{9,10},{10,1... | collective-permute-start | bytes 1179656 | tf_op jit(solution)/shard_map/ppermute | solution.py:523
  22.3 24.7 %collective-permute-start.2 = (bf16[4,96,896]{2,1,0:T(8,128)(2,1)S(1)}, bf16[4,96,896]{2,1,0:T(8,128)(2,1)S(1)}, u32[]{:S(2)}, u32[]{:S(2)}) collective-permute-start(bf16[4,96,896]{2,1,0:T(8,128)(2,1)S(1)} %pad_maximum_fusion.1.near), channel_id=1, source_target_pairs={{0,4},{4,0},{8,12},{12,8},{16,20},{20,16},{24,28},{28,24},{1,5},{5... | collective-permute-start | bytes 2064392 | tf_op jit(solution)/shard_map/ppermute | solution.py:527
  22.5 23.2 %collective-permute-start.13 = (bf16[1344,128]{1,0:T(8,128)(2,1)S(1)}, bf16[1344,128]{1,0:T(8,128)(2,1)}, u32[]{:S(2)}, u32[]{:S(2)}) collective-permute-start(bf16[1344,128]{1,0:T(8,128)(2,1)S(1)} %pad_maximum_fusion.3.p0), channel_id=1, source_target_pairs={{0,1},{1,2},{2,3},{3,0},{4,5},{5,6},{6,7},{7,4},{8,9},{9,10},{10,1... | collective-permute-start | bytes 1032200 | tf_op jit(solution)/shard_map/ppermute | solution.py:523
  29.8 24.3 %collective-permute-start.5 = (bf16[256,768]{1,0:T(8,128)(2,1)S(1)}, bf16[256,768]{1,0:T(8,128)(2,1)}, u32[]{:S(2)}, u32[]{:S(2)}) collective-permute-start(bf16[256,768]{1,0:T(8,128)(2,1)S(1)} %collective-permute-done.3.xa), channel_id=1, source_target_pairs={{0,1},{1,2},{2,3},{3,0},{4,5},{5,6},{6,7},{7,4},{8,9},{9,10},{10,1... | collective-permute-start | bytes 1179656 | tf_op jit(solution)/shard_map/ppermute | solution.py:523
  45.7 15.8 %collective-permute-start.14 = (bf16[1344,128]{1,0:T(8,128)(2,1)}, bf16[1344,128]{1,0:T(8,128)(2,1)}, u32[]{:S(2)}, u32[]{:S(2)}) collective-permute-start(bf16[1344,128]{1,0:T(8,128)(2,1)} %collective-permute-done.13.p1), channel_id=1, source_target_pairs={{0,1},{1,2},{2,3},{3,0},{4,5},{5,6},{6,7},{7,4},{8,9},{9,10},{10,1... | collective-permute-start | bytes 1032200 | tf_op jit(solution)/shard_map/ppermute | solution.py:523
  45.7 24.1 %collective-permute-start.6 = (bf16[256,768]{1,0:T(8,128)(2,1)}, bf16[256,768]{1,0:T(8,128)(2,1)S(1)}, u32[]{:S(2)}, u32[]{:S(2)}) collective-permute-start(bf16[256,768]{1,0:T(8,128)(2,1)} %collective-permute-done.4.xb), channel_id=1, source_target_pairs={{0,1},{1,2},{2,3},{3,0},{4,5},{5,6},{6,7},{7,4},{8,9},{9,10},{10,1... | collective-permute-start | bytes 1179656 | tf_op jit(solution)/shard_map/ppermute | solution.py:523
  80.0 19.4 %collective-permute-start.16 = (bf16[4,768,128]{2,1,0:T(8,128)(2,1)}, bf16[4,768,128]{2,1,0:T(8,128)(2,1)S(1)}, u32[]{:S(2)}, u32[]{:S(2)}) collective-permute-start(bf16[4,768,128]{2,1,0:T(8,128)(2,1)} %get-tuple-element.90.refs_0_), channel_id=1, source_target_pairs={{0,8},{4,12},{8,0},{12,4},{16,24},{20,28},{24,16},{28,20},{1,9},{5... | collective-permute-start | bytes 2359304 | tf_op jit(solution)/shard_map/ppermute | solution.py:527
  81.5 19.9 %collective-permute-start.19 = (bf16[4,576,128]{2,1,0:T(8,128)(2,1)}, bf16[4,576,128]{2,1,0:T(8,128)(2,1)S(1)}, u32[]{:S(2)}, u32[]{:S(2)}) collective-permute-start(bf16[4,576,128]{2,1,0:T(8,128)(2,1)} %get-tuple-element.94.refs_4_), channel_id=1, source_target_pairs={{0,16},{4,20},{8,24},{12,28},{16,0},{20,4},{24,8},{28,12},{1,17},{... | collective-permute-start | bytes 1769480 | tf_op jit(solution)/shard_map/ppermute | solution.py:527
  82.0 20.9 %collective-permute-start.7 = (bf16[256,768]{1,0:T(8,128)(2,1)}, bf16[256,768]{1,0:T(8,128)(2,1)S(1)}, u32[]{:S(2)}, u32[]{:S(2)}) collective-permute-start(bf16[256,768]{1,0:T(8,128)(2,1)} %collective-permute-done.5.xa), channel_id=1, source_target_pairs={{0,1},{1,2},{2,3},{3,0},{4,5},{5,6},{6,7},{7,4},{8,9},{9,10},{10,1... | collective-permute-start | bytes 1179656 | tf_op jit(solution)/shard_map/ppermute | solution.py:523
  82.0 24.0 %collective-permute-start.8 = (bf16[256,768]{1,0:T(8,128)(2,1)S(1)}, bf16[256,768]{1,0:T(8,128)(2,1)}, u32[]{:S(2)}, u32[]{:S(2)}) collective-permute-start(bf16[256,768]{1,0:T(8,128)(2,1)S(1)} %collective-permute-done.6.xb), channel_id=1, source_target_pairs={{0,1},{1,2},{2,3},{3,0},{4,5},{5,6},{6,7},{7,4},{8,9},{9,10},{10,1... | collective-permute-start | bytes 1179656 | tf_op jit(solution)/shard_map/ppermute | solution.py:523
  99.3 29.3 %collective-permute-start.18 = (bf16[4,768,128]{2,1,0:T(8,128)(2,1)S(1)}, bf16[4,768,128]{2,1,0:T(8,128)(2,1)S(1)}, u32[]{:S(2)}, u32[]{:S(2)}) collective-permute-start(bf16[4,768,128]{2,1,0:T(8,128)(2,1)S(1)} %collective-permute-done.16.refs_1_), channel_id=1, source_target_pairs={{0,16},{4,20},{8,24},{12,28},{16,0},{20,4},{24,8},{28,12},{1,17},{... | collective-permute-start | bytes 2359304 | tf_op jit(solution)/shard_map/ppermute | solution.py:527
  100.1 34.6 %collective-permute-start.17 = (bf16[4,768,128]{2,1,0:T(8,128)(2,1)}, bf16[4,768,128]{2,1,0:T(8,128)(2,1)}, u32[]{:S(2)}, u32[]{:S(2)}) collective-permute-start(bf16[4,768,128]{2,1,0:T(8,128)(2,1)} %get-tuple-element.90.refs_0_), channel_id=1, source_target_pairs={{0,16},{4,20},{8,24},{12,28},{16,0},{20,4},{24,8},{28,12},{1,17},{... | collective-permute-start | bytes 2359304 | tf_op jit(solution)/shard_map/ppermute | solution.py:527
  101.4 27.3 %collective-permute-start.20 = (bf16[4,576,128]{2,1,0:T(8,128)(2,1)}, bf16[4,576,128]{2,1,0:T(8,128)(2,1)}, u32[]{:S(2)}, u32[]{:S(2)}) collective-permute-start(bf16[4,576,128]{2,1,0:T(8,128)(2,1)} %get-tuple-element.94.refs_4_), channel_id=1, source_target_pairs={{0,8},{4,12},{8,0},{12,4},{16,24},{20,28},{24,16},{28,20},{1,9},{5... | collective-permute-start | bytes 1769480 | tf_op jit(solution)/shard_map/ppermute | solution.py:527
  102.9 25.0 %collective-permute-start.21 = (bf16[4,576,128]{2,1,0:T(8,128)(2,1)S(1)}, bf16[4,576,128]{2,1,0:T(8,128)(2,1)S(1)}, u32[]{:S(2)}, u32[]{:S(2)}) collective-permute-start(bf16[4,576,128]{2,1,0:T(8,128)(2,1)S(1)} %collective-permute-done.19.refs_5_), channel_id=1, source_target_pairs={{0,8},{4,12},{8,0},{12,4},{16,24},{20,28},{24,16},{28,20},{1,9},{5... | collective-permute-start | bytes 1769480 | tf_op jit(solution)/shard_map/ppermute | solution.py:527
  140.7 17.9 %collective-permute-start.22 = (bf16[4,4,96,256]{3,2,1,0:T(8,128)(2,1)}, bf16[4,4,96,256]{3,2,1,0:T(8,128)(2,1)S(1)}, u32[]{:S(2)}, u32[]{:S(2)}) collective-permute-start(bf16[4,4,96,256]{3,2,1,0:T(8,128)(2,1)} %get-tuple-element.97.near), channel_id=1, source_target_pairs={{0,4},{4,0},{8,12},{12,8},{16,20},{20,16},{24,28},{28,24},{1,5},{5... | collective-permute-start | bytes 2359304 | tf_op jit(solution)/shard_map/ppermute | solution.py:527
  141.4 17.1 %collective-permute-start.10 = (bf16[192,512]{1,0:T(8,128)(2,1)S(1)}, bf16[192,512]{1,0:T(8,128)(2,1)S(1)}, u32[]{:S(2)}, u32[]{:S(2)}) collective-permute-start(bf16[192,512]{1,0:T(8,128)(2,1)S(1)} %get-tuple-element.159), channel_id=1, source_target_pairs={{0,2},{1,3},{2,0},{3,1},{4,6},{5,7},{6,4},{7,5},{8,10},{9,11},{10,... | collective-permute-start | bytes 589832 | tf_op jit(solution)/shard_map/ppermute | solution.py:523
  145.4 20.7 %collective-permute-start.24 = (bf16[512,768]{1,0:T(8,128)(2,1)S(1)}, bf16[512,768]{1,0:T(8,128)(2,1)S(1)}, u32[]{:S(2)}, u32[]{:S(2)}) collective-permute-start(bf16[512,768]{1,0:T(8,128)(2,1)S(1)} %copy-done.14), channel_id=1, source_target_pairs={{0,4},{4,0},{8,12},{12,8},{16,20},{20,16},{24,28},{28,24},{1,5},{5... | collective-permute-start | bytes 2359304 | tf_op jit(solution)/shard_map/ppermute | solution.py:527
  203.3 17.4 %collective-permute-start.29 = (bf16[192,512]{1,0:T(8,128)(2,1)S(1)}, bf16[192,512]{1,0:T(8,128)(2,1)S(1)}, u32[]{:S(2)}, u32[]{:S(2)}) collective-permute-start(bf16[192,512]{1,0:T(8,128)(2,1)S(1)} %get-tuple-element.154), channel_id=1, source_target_pairs={{0,2},{1,3},{2,0},{3,1},{4,6},{5,7},{6,4},{7,5},{8,10},{9,11},{10,... | collective-permute-start | bytes 589832 | tf_op jit(solution)/shard_map/ppermute | solution.py:523
  206.5 16.5 %collective-permute-start.26 = (bf16[192,512]{1,0:T(8,128)(2,1)S(1)}, bf16[192,512]{1,0:T(8,128)(2,1)S(1)}, u32[]{:S(2)}, u32[]{:S(2)}) collective-permute-start(bf16[192,512]{1,0:T(8,128)(2,1)S(1)} %get-tuple-element.157), channel_id=1, source_target_pairs={{0,1},{1,2},{2,3},{3,0},{4,5},{5,6},{6,7},{7,4},{8,9},{9,10},{10,1... | collective-permute-start | bytes 589832 | tf_op jit(solution)/shard_map/ppermute | solution.py:523
  208.1 16.3 %collective-permute-start.28 = (bf16[192,512]{1,0:T(8,128)(2,1)S(1)}, bf16[192,512]{1,0:T(8,128)(2,1)S(1)}, u32[]{:S(2)}, u32[]{:S(2)}) collective-permute-start(bf16[192,512]{1,0:T(8,128)(2,1)S(1)} %get-tuple-element.155), channel_id=1, source_target_pairs={{0,3},{1,0},{2,1},{3,2},{4,7},{5,4},{6,5},{7,6},{8,11},{9,8},{10,9... | collective-permute-start | bytes 589832 | tf_op jit(solution)/shard_map/ppermute | solution.py:523
  224.1 19.0 %collective-permute-start.30 = (bf16[4,96,1024]{2,1,0:T(8,128)(2,1)}, bf16[4,96,1024]{2,1,0:T(8,128)(2,1)}, u32[]{:S(2)}, u32[]{:S(2)}) collective-permute-start(bf16[4,96,1024]{2,1,0:T(8,128)(2,1)} %dynamic-slice_bitcast_fusion.1), channel_id=1, source_target_pairs={{0,4},{4,0},{8,12},{12,8},{16,20},{20,16},{24,28},{28,24},{1,5},{5... | collective-permute-start | bytes 2359304 | tf_op jit(solution)/shard_map/ppermute | solution.py:527
  230.0 66.7 %collective-permute-start.40 = (bf16[4,96,1536]{2,1,0:T(8,128)(2,1)}, bf16[4,96,1536]{2,1,0:T(8,128)(2,1)}, u32[]{:S(2)}, u32[]{:S(2)}) collective-permute-start(bf16[4,96,1536]{2,1,0:T(8,128)(2,1)} %dynamic-slice_bitcast_fusion), channel_id=1, source_target_pairs={{0,16},{4,20},{8,24},{12,28},{16,0},{20,4},{24,8},{28,12},{1,17},{... | collective-permute-start | bytes 3538952 | tf_op jit(solution)/shard_map/ppermute | solution.py:527
  278.0 29.2 %collective-permute-start.41 = (bf16[4,96,1536]{2,1,0:T(8,128)(2,1)}, bf16[4,96,1536]{2,1,0:T(8,128)(2,1)}, u32[]{:S(2)}, u32[]{:S(2)}) collective-permute-start(bf16[4,96,1536]{2,1,0:T(8,128)(2,1)} %bitcast.38), channel_id=1, source_target_pairs={{0,8},{4,12},{8,0},{12,4},{16,24},{20,28},{24,16},{28,20},{1,9},{5... | collective-permute-start | bytes 3538952 | tf_op jit(solution)/shard_map/ppermute | solution.py:527
  279.3 44.1 %collective-permute-start.34 = (bf16[256,768]{1,0:T(8,128)(2,1)}, bf16[256,768]{1,0:T(8,128)(2,1)}, u32[]{:S(2)}, u32[]{:S(2)}) collective-permute-start(bf16[256,768]{1,0:T(8,128)(2,1)} %get-tuple-element.153), channel_id=1, source_target_pairs={{0,1},{1,2},{2,3},{3,0},{4,5},{5,6},{6,7},{7,4},{8,9},{9,10},{10,1... | collective-permute-start | bytes 1179656 | tf_op jit(solution)/shard_map/ppermute | solution.py:523
  281.7 32.2 %collective-permute-start.42 = (bf16[2,96,1024]{2,1,0:T(8,128)(2,1)}, bf16[2,96,1024]{2,1,0:T(8,128)(2,1)}, u32[]{:S(2)}, u32[]{:S(2)}) collective-permute-start(bf16[2,96,1024]{2,1,0:T(8,128)(2,1)} %get-tuple-element.123), channel_id=1, source_target_pairs={{0,8},{4,12},{8,0},{12,4},{16,24},{20,28},{24,16},{28,20},{1,9},{5... | collective-permute-start | bytes 1179656 | tf_op jit(solution)/shard_map/ppermute | solution.py:527
  290.7 32.7 %collective-permute-start.32 = (bf16[256,768]{1,0:T(8,128)(2,1)}, bf16[256,768]{1,0:T(8,128)(2,1)}, u32[]{:S(2)}, u32[]{:S(2)}) collective-permute-start(bf16[256,768]{1,0:T(8,128)(2,1)} %fusion.19), channel_id=1, source_target_pairs={{0,1},{1,2},{2,3},{3,0},{4,5},{5,6},{6,7},{7,4},{8,9},{9,10},{10,1... | collective-permute-start | bytes 1179656 | tf_op jit(solution)/shard_map/ppermute | solution.py:523
  319.4 19.2 %collective-permute-start.44 = (bf16[4,768,128]{2,1,0:T(8,128)(2,1)}, bf16[4,768,128]{2,1,0:T(8,128)(2,1)}, u32[]{:S(2)}, u32[]{:S(2)}) collective-permute-start(bf16[4,768,128]{2,1,0:T(8,128)(2,1)} %get-tuple-element.128), channel_id=1, source_target_pairs={{0,16},{4,20},{8,24},{12,28},{16,0},{20,4},{24,8},{28,12},{1,17},{... | collective-permute-start | bytes 2359304 | tf_op jit(solution)/shard_map/ppermute | solution.py:527
  321.9 29.2 %collective-permute-start.37 = (bf16[4,96,768]{2,1,0:T(8,128)(2,1)}, bf16[4,96,768]{2,1,0:T(8,128)(2,1)}, u32[]{:S(2)}, u32[]{:S(2)}) collective-permute-start(bf16[4,96,768]{2,1,0:T(8,128)(2,1)} %dynamic-slice_bitcast_fusion.2), channel_id=1, source_target_pairs={{0,4},{4,0},{8,12},{12,8},{16,20},{20,16},{24,28},{28,24},{1,5},{5... | collective-permute-start | bytes 1769480 | tf_op jit(solution)/shard_map/ppermute | solution.py:527
  321.9 16.0 %collective-permute-start.43 = (bf16[4,576,128]{2,1,0:T(8,128)(2,1)}, bf16[4,576,128]{2,1,0:T(8,128)(2,1)S(1)}, u32[]{:S(2)}, u32[]{:S(2)}) collective-permute-start(bf16[4,576,128]{2,1,0:T(8,128)(2,1)} %get-tuple-element.125), channel_id=1, source_target_pairs={{0,8},{4,12},{8,0},{12,4},{16,24},{20,28},{24,16},{28,20},{1,9},{5... | collective-permute-start | bytes 1769480 | tf_op jit(solution)/shard_map/ppermute | solution.py:527
  342.0 24.5 %collective-permute-start.45 = (bf16[1344,128]{1,0:T(8,128)(2,1)}, bf16[1344,128]{1,0:T(8,128)(2,1)}, u32[]{:S(2)}, u32[]{:S(2)}) collective-permute-start(bf16[1344,128]{1,0:T(8,128)(2,1)} %get-tuple-element.129), channel_id=1, source_target_pairs={{0,1},{1,2},{2,3},{3,0},{4,5},{5,6},{6,7},{7,4},{8,9},{9,10},{10,1... | collective-permute-start | bytes 1032200 | tf_op jit(solution)/shard_map/ppermute | solution.py:523
  351.1 16.9 %collective-permute-start.27 = (bf16[512,768]{1,0:T(8,128)(2,1)}, bf16[512,768]{1,0:T(8,128)(2,1)S(1)}, u32[]{:S(2)}, u32[]{:S(2)}) collective-permute-start(bf16[512,768]{1,0:T(8,128)(2,1)} %out_far.1), channel_id=1, source_target_pairs={{0,4},{4,0},{8,12},{12,8},{16,20},{20,16},{24,28},{28,24},{1,5},{5... | collective-permute-start | bytes 2359304 | tf_op jit(solution)/shard_map/ppermute | solution.py:527
  371.2 29.8 %collective-permute-start.33 = (bf16[256,768]{1,0:T(8,128)(2,1)S(1)}, bf16[256,768]{1,0:T(8,128)(2,1)}, u32[]{:S(2)}, u32[]{:S(2)}) collective-permute-start(bf16[256,768]{1,0:T(8,128)(2,1)S(1)} %get-tuple-element.146), channel_id=1, source_target_pairs={{0,1},{1,2},{2,3},{3,0},{4,5},{5,6},{6,7},{7,4},{8,9},{9,10},{10,1... | collective-permute-start | bytes 1179656 | tf_op jit(solution)/shard_map/ppermute | solution.py:523
  (71 other events, 741.5 us)
